TPU v7x, 128 devices: a whole 4x4x4 slice. The times are simulated.
128 devices in a mesh: group: 8 (over z, core), member: 16 (over x, y).
Axes of the slice: x: 4, y: 4, z: 4, core: 2. Of those that a mesh axis runs over, the one named last changes fastest.
Arguments:
- hidden: bfloat16 [12288, 2048], P('group'), may hold values from -6 to 6
- token_slab: int32 [12288, 1], P(('group', 'member')), may hold values from 0 to 127; in each aligned block of 96 rows (0 to 95, 96 to 191, ...) at most 2 rows name the same one
- token_row: int32 [12288], P(('group', 'member')), may hold values from 0 to 2047
- slab_owner: int32 [128], replicated, may hold values from 0 to 127, each once
- ple_table: bfloat16 [262144, 256], P(('group', 'member')), may hold values from -0.375 to 0.375
- norm_gains: float32 [1, 3, 2048], replicated, may hold values from 0.1 to 1.9
- w_gate: bfloat16 [1, 2048, 8192], P(None, None, 'member'), may hold values from -0.125 to 0.125
- w_up: bfloat16 [1, 2048, 8192], P(None, None, 'member'), may hold values from -0.125 to 0.125
- w_down: bfloat16 [1, 8192, 2048], P(None, 'member'), may hold values from -0.0625 to 0.0625
- ple_gate: bfloat16 [1, 2048, 256], P(None, None, 'member'), may hold values from -0.125 to 0.125
- ple_proj: bfloat16 [1, 256, 2048], P(None, 'member'), may hold values from -0.375 to 0.375
Outputs:
- hidden_out: bfloat16 [12288, 2048], P('group')
Inputs may be any that keep to these rules, and one draw needn't show every extreme that they name: Within the 96 tokens of one device (aligned blocks of token_slab), no slab is named by more than 2 tokens. Each number appears once: slab s is stored in rows slab_owner[s] * 2048 to slab_owner[s] * 2048 + 2047 of ple_table.
All inputs are finite; a program needn't handle non-finite values.
Results may differ from a plain program's by a relative error of at most 0.0061.
Values may be sent and summed in bfloat16 or wider, within the bound.
A program may use at most 128 MiB of HBM per device.

v0:
```python
import jax
import jax.numpy as jnp
from jax import lax
from jax.sharding import PartitionSpec as P

PLE = 256


epsilon = 1e-06


def in_blocks(x, dim, devices):
    shape = x.shape
    parts = x.reshape(*shape[:dim], devices, shape[dim] // devices, *shape[dim + 1 :])
    return jnp.moveaxis(parts, dim, 0)


def joined_along(parts, dim):
    shape = list(parts.shape[1:])
    shape[dim] *= parts.shape[0]
    return jnp.moveaxis(parts, 0, dim).reshape(shape)


def exchange_both(x, axis, axes, splits, concats):
    sizes = [lax.axis_size(a) for a in axes]
    parts = in_blocks(x, splits[0], sizes[0])
    parts = jnp.moveaxis(in_blocks(parts, splits[1] + 1, sizes[1]), 0, 1)
    inside = parts.shape[2:]
    parts = parts.reshape(-1, *inside)
    parts = lax.all_to_all(parts, axis, split_axis=0, concat_axis=0, tiled=True)
    parts = joined_along(parts.reshape(*sizes, *inside), concats[0] + 1)
    return joined_along(parts, concats[1])


def norm_rows(values, scales):
    return values * lax.rsqrt(jnp.mean(values * values, axis=-1, keepdims=True) + epsilon) * scales


def lookup_rows(wanted, ple_table):
    flat_ids = wanted.reshape(-1) - 1
    one_hot = (
        flat_ids[:, None] == jnp.arange(ple_table.shape[0], dtype=jnp.int32)[None, :]
    ).astype(jnp.bfloat16)
    served = jnp.dot(one_hot, ple_table, preferred_element_type=jnp.float32).astype(jnp.bfloat16)
    return served.reshape(wanted.shape + (ple_table.shape[1],))


def request_slots(slab_ids, token_row, slab_owner, devices, slots):
    target = slab_owner[slab_ids]
    order = jnp.arange(token_row.shape[0], dtype=jnp.int32)
    earlier = (target[None, :] == target[:, None]) & (order[None, :] < order[:, None])
    slot_of = jnp.sum(earlier.astype(jnp.int32), axis=1)
    hit_map = (target[:, None, None] == jnp.arange(devices, dtype=jnp.int32)[None, :, None]) & (
        slot_of[:, None, None] == jnp.arange(slots, dtype=jnp.int32)[None, None, :]
    )
    requests = jnp.sum(jnp.where(hit_map, token_row[:, None, None] + 1, 0), axis=0)
    return (hit_map, requests)


def pick_rows(hit_map, returned):
    return jnp.einsum(
        "tdc,dcw->tw", hit_map.astype(jnp.bfloat16), returned, preferred_element_type=jnp.float32
    ).astype(jnp.bfloat16)


def combine_branch(current, partial_value, scales):
    summed = lax.psum(partial_value, "member")
    return current + norm_rows(summed, scales)


def per_device(
    hidden,
    token_slab,
    token_row,
    slab_owner,
    ple_table,
    norm_gains,
    w_gate,
    w_up,
    w_down,
    ple_gate,
    ple_proj,
):
    members = lax.axis_size("member")
    devices = lax.axis_size("group") * members
    tokens_here = token_row.shape[0]
    slots = max(2, (2 * tokens_here + devices - 1) // devices)
    slab_ids = token_slab[:, 0]
    hit_map, requests = request_slots(slab_ids, token_row, slab_owner, devices, slots)
    grouped = requests.reshape(lax.axis_size("group"), members, slots)
    received = lax.all_to_all(
        lax.all_to_all(grouped, "group", split_axis=0, concat_axis=0, tiled=True),
        "member",
        split_axis=1,
        concat_axis=1,
        tiled=True,
    )
    served = lookup_rows(received, ple_table)
    returned = exchange_both(served, ("group", "member"), ("group", "member"), (0, 1), (0, 1))
    own_rows = pick_rows(hit_map, returned.reshape(devices, slots, ple_table.shape[1]))
    per_member = ple_gate.shape[2]
    layers = w_gate.shape[0]
    pieces = own_rows.reshape(tokens_here, layers, members, per_member)
    columns = lax.all_to_all(pieces, "member", split_axis=2, concat_axis=0, tiled=True)
    ple_part = columns.reshape(-1, layers, per_member).astype(jnp.float32) * PLE**0.5
    current = hidden.astype(jnp.float32)
    normed = norm_rows(current, norm_gains[0, 0]).astype(jnp.bfloat16)
    gate_part = jnp.dot(normed, w_gate[0], preferred_element_type=jnp.float32)
    up_part = jnp.dot(normed, w_up[0], preferred_element_type=jnp.float32)
    activated = (jax.nn.gelu(gate_part, approximate=True) * up_part).astype(jnp.bfloat16)
    mlp_out = jnp.dot(activated, w_down[0], preferred_element_type=jnp.float32)
    current = combine_branch(current, mlp_out, norm_gains[0, 1])
    current_b = current.astype(jnp.bfloat16)
    ple_gate_out = jnp.dot(current_b, ple_gate[0], preferred_element_type=jnp.float32)
    ple_act = (jax.nn.gelu(ple_gate_out, approximate=True) * ple_part[:, 0, :]).astype(jnp.bfloat16)
    ple_out = jnp.dot(ple_act, ple_proj[0], preferred_element_type=jnp.float32)
    current = combine_branch(current, ple_out, norm_gains[0, 2])
    return current.astype(jnp.bfloat16)


def solution(mesh):
    return jax.shard_map(
        per_device,
        mesh=mesh,
        in_specs=(
            P("group", None),
            P(("group", "member"), None),
            P(("group", "member")),
            P(),
            P(("group", "member"), None),
            P(),
            P(None, None, "member"),
            P(None, None, "member"),
            P(None, "member", None),
            P(None, None, "member"),
            P(None, "member", None),
        ),
        out_specs=P("group", None),
        check_vma=False,
    )
```

profile of v0, /device:TPU:0, one launch (start us, length us, event | category | flops | bytes accessed | tf_op | source)
XLA Modules:
  0.0 437.0 jit_solution(8497324638105972487)
XLA Ops:
  6.5 4.2 fusion
  10.8 0.5 copy-done.3
  11.3 6.8 %fusion.17 = f32[1536,512]{1,0:T(8,128)} fusion(bf16[1,2048,512]{2,1,0:T(8,128)(2,1)} %param.17, bf16[1536,2048]{1,0:T(8,128)(2,1)S(1)} %copy-done.3, f32[2048]{0:T(1024)S(1)} %bitcast.58, f32[1536]{0:T(1024)S(1)} %add_rsqrt_fusion.2), kind=kOutput, calls=%fused_computation.25 | convolution fusion | flops 3233808384 | bytes 11548672 | tf_op jit(solution)/shard_map/dot_general | solution.py:108
  18.1 13.3 %fusion.14 = f32[1536,2048]{1,0:T(8,128)} fusion(bf16[1,512,2048]{2,1,0:T(8,128)(2,1)S(1)} %copy-done, f32[1536,512]{1,0:T(8,128)} %fusion.17, bf16[1,2048,512]{2,1,0:T(8,128)(2,1)} %param.18, bf16[1536,2048]{1,0:T(8,128)(2,1)} %param.11, f32[2048]{0:T(1024)S(1)} %bitcast.59, f32[1536]{0:T(1024)S(1)} %add_rsqrt_fusion.2), kind=kOutput, calls=%fused_computation.22 | convolution fusion | flops 6462898176 | bytes 26228736 | tf_op jit(solution)/shard_map/dot_general | solution.py:111
  31.5 0.6 copy-done.9
  32.1 1.2 gather_fusion
  33.3 0.2 convert_reduce_fusion
  33.6 0.1 fusion.30
  33.8 10.5 %all_to_all.24 = s32[8,16,2]{1,2,0:T(2,128)S(1)} all-to-all(s32[8,16,2]{1,2,0:T(2,128)S(1)} %copy.33), channel_id=1, replica_groups=mesh['group'=8,'member'=16] {'group'}, dimensions={0} | all-to-all | bytes 2048 | tf_op jit(solution)/shard_map/all_to_all | solution.py:92
  44.4 14.6 %all_to_all.25 = s32[8,16,2]{0,2,1:T(2,128)S(1)} all-to-all(s32[8,16,2]{0,2,1:T(2,128)S(1)} %copy.34), channel_id=1, replica_groups=mesh['group'=8,'member'=16] {'member'}, dimensions={1} | all-to-all | bytes 2048 | tf_op jit(solution)/shard_map/all_to_all | solution.py:91
  59.1 0.1 copy.36
  59.2 0.1 sub.7
  59.4 0.5 fusion.26
  60.0 15.6 %all_to_all.26 = bf16[128,1,1,2,256]{4,3,2,1,0:T(2,128)(2,1)S(1)} all-to-all(bf16[128,1,1,2,256]{4,3,2,1,0:T(2,128)(2,1)S(1)} %bitcast.52), channel_id=1, replica_groups=mesh['group'=8,'member'=16] {'group','member'}, dimensions={0} | all-to-all | bytes 262144 | tf_op jit(solution)/shard_map/all_to_all | solution.py:30
  75.5 0.2 fusion.27
  75.8 0.1 copy.39
  75.9 11.2 %all_to_all.27 = bf16[96,1,16,16]{0,3,1,2:T(8,128)(2,1)S(1)} all-to-all(bf16[96,1,16,16]{0,3,1,2:T(8,128)(2,1)S(1)} %bitcast.54), channel_id=1, replica_groups=mesh['group'=8,'member'=16] {'member'}, dimensions={2} | all-to-all | bytes 98304 | tf_op jit(solution)/shard_map/all_to_all | solution.py:104
  87.3 127.7 %all-reduce.3.cloned.1.call-done = f32[1536,2048]{1,0:T(8,128)} async-done(((f32[1536,2048]{1,0:T(8,128)}), f32[1536,2048]{1,0:T(8,128)}) %all-reduce.3.cloned.1.call-update) | async-done | bytes 12582928 | tf_op jit(solution)/shard_map/psum | solution.py:67
  215.0 5.5 %multiply_reduce_fusion.1 = f32[1536]{0:T(1024)S(1)} fusion(f32[1536,2048]{1,0:T(8,128)} %all-reduce.3.cloned.1.call-done), kind=kLoop, calls=%fused_computation.9 | loop fusion | flops 6289920 | bytes 12589056 | tf_op jit(solution)/shard_map/reduce_sum | solution.py:36
  220.5 11.5 %fusion.47 = f32[1536,2048]{1,0:T(8,128)} fusion(f32[1536,16]{0,1:T(8,128)S(1)} %mul.160, f32[1536,2048]{1,0:T(8,128)} %all-reduce.3.cloned.1.call-done, bf16[1536,2048]{1,0:T(8,128)(2,1)} %param.11, f32[2048]{0:T(1024)S(1)} %bitcast.55, f32[1536]{0:T(1024)S(1)} %add_rsqrt_fusion.1, bf16[1,16,2048]{2,1,0:T(8,128)(2,1)S(1)} %copy-done.5, ...), kind=kOutput, calls=%fused_computation.47 | convolution fusion | flops 217300992 | bytes 31700992 | tf_op jit(solution)/shard_map/dot_general | solution.py:116
  232.0 178.6 %all-reduce.5.cloned.1.call-done = f32[1536,2048]{1,0:T(8,128)} async-done(((f32[1536,2048]{1,0:T(8,128)}), f32[1536,2048]{1,0:T(8,128)}) %all-reduce.5.cloned.1.call-update) | async-done | bytes 12582928 | tf_op jit(solution)/shard_map/psum | solution.py:67
  410.7 5.6 %multiply_reduce_fusion = f32[1536]{0:T(1024)S(1)} fusion(f32[1536,2048]{1,0:T(8,128)} %all-reduce.5.cloned.1.call-done), kind=kLoop, calls=%fused_computation.8 | loop fusion | flops 6289920 | bytes 12589056 | tf_op jit(solution)/shard_map/reduce_sum | solution.py:36
  416.3 2.5 copy-done.4
  418.8 11.3 %add_convert_fusion = bf16[1536,2048]{1,0:T(8,128)(2,1)} fusion(f32[1536,2048]{1,0:T(8,128)S(1)} %copy-done.4, f32[1536,2048]{1,0:T(8,128)} %all-reduce.3.cloned.1.call-done, bf16[1536,2048]{1,0:T(8,128)(2,1)} %param.11, f32[2048]{0:T(1024)S(1)} %bitcast.57, f32[1536]{0:T(1024)S(1)} %add_rsqrt_fusion, f32[2048]{0:T(1024)S(1)} %bitcast.56, ...), kind=kLoop, calls=%fused_computation.7 | loop fusion | flops 25165824 | bytes 37777408 | tf_op jit(solution)/shard_map/convert_element_type | solution.py:118
  (42 shorter events, 0.7 us)
Async XLA Ops:
  6.5 11.6 %copy-start = (bf16[1,512,2048]{2,1,0:T(8,128)(2,1)S(1)}, bf16[1,512,2048]{2,1,0:T(8,128)(2,1)}, u32[]{:S(2)}) copy-start(bf16[1,512,2048]{2,1,0:T(8,128)(2,1)} %param.19) | copy-start | bytes 6291460
  6.5 4.3 copy-start.7
  6.5 208.4 %all-reduce.3.cloned.1.call-start = ((), (), s32[]{:S(2)}) async-start(), calls=%async_computation.4 | async-start | bytes 25165824 | tf_op jit(solution)/shard_map/psum | solution.py:67
  6.5 4.8 %copy-start.3 = (bf16[1536,2048]{1,0:T(8,128)(2,1)S(1)}, bf16[1536,2048]{1,0:T(8,128)(2,1)}, u32[]{:S(2)}) copy-start(bf16[1536,2048]{1,0:T(8,128)(2,1)} %param.11) | copy-start | bytes 18874372
  31.4 0.7 copy-start.9
  31.4 0.7 copy-start.2
  31.4 2.1 copy-start.10
  31.4 28.0 %copy-start.8 = (bf16[2048,256]{1,0:T(8,128)(2,1)S(1)}, bf16[2048,256]{1,0:T(8,128)(2,1)}, u32[]{:S(2)}) copy-start(bf16[2048,256]{1,0:T(8,128)(2,1)} %param.15) | copy-start | bytes 3145732
  31.5 379.2 %all-reduce.5.cloned.1.call-start = ((), (), s32[]{:S(2)}) async-start(), calls=%async_computation.5 | async-start | bytes 25165824 | tf_op jit(solution)/shard_map/psum | solution.py:67
  87.3 133.2 %copy-start.5 = (bf16[1,16,2048]{2,1,0:T(8,128)(2,1)S(1)}, bf16[1,16,2048]{2,1,0:T(8,128)(2,1)}, u32[]{:S(2)}) copy-start(bf16[1,16,2048]{2,1,0:T(8,128)(2,1)} %param.21) | copy-start | bytes 196612
  87.3 133.2 %copy-start.6 = (bf16[1,2048,16]{1,2,0:T(8,128)(2,1)S(1)}, bf16[1,2048,16]{1,2,0:T(8,128)(2,1)}, u32[]{:S(2)}) copy-start(bf16[1,2048,16]{1,2,0:T(8,128)(2,1)} %param.20) | copy-start | bytes 196612
  410.7 8.2 %copy-start.4 = (f32[1536,2048]{1,0:T(8,128)S(1)}, f32[1536,2048]{1,0:T(8,128)}, u32[]{:S(2)}) copy-start(f32[1536,2048]{1,0:T(8,128)} %all-reduce.5.cloned.1.call-done) | copy-start | bytes 37748740
  418.8 11.3 %copy-start.1 = (bf16[1,512,2048]{2,1,0:T(8,128)(2,1)S(1)}, bf16[1,512,2048]{2,1,0:T(8,128)(2,1)}, u32[]{:S(2)}) copy-start(bf16[1,512,2048]{2,1,0:T(8,128)(2,1)} %param.19) | copy-start | bytes 6291460
Sparse Core Ops, SparseCore 0:
  31.6 183.3 all-reduce.2
  232.2 178.4 all-reduce.4
where the time goes:
time: 438 us; the launch traced here: 437 us
  waiting for transfers between devices  306 us (70%)
  blocking collectives  51.9 us (12%)
  matrix products  32.3 us (7%)
  other arithmetic  27 us (6%)
  between operations  13.6 us (3%)
  local copies, waits for them, and re-layouts  5.69 us (1%)
    psum x2, waiting for transfers between devices, combine_branch(): summed = lax.psum(partial_value, 'member')  306 us
    all_to_all x1, blocking collectives, exchange_both(): parts = lax.all_to_all(parts, axis, split_axis=0, concat_axis=0, tiled=True)  15.6 us
    reduce_sum x3, other arithmetic, norm_rows(): jnp.mean(values * values, axis=-1, keepdims=True) + epsilon  15.3 us
    all_to_all x1, blocking collectives, per_device(): lax.all_to_all(lax.all_to_all(grouped, 'group', split_axis=0, concat_axis...  14.6 us
    dot_general x1, matrix products, per_device(): mlp_out = jnp.dot(activated, w_down[0], preferred_element_type=jnp.float32)  13.3 us
    dot_general x1, matrix products, per_device(): ple_out = jnp.dot(ple_act, ple_proj[0], preferred_element_type=jnp.float32)  11.5 us
    convert_element_type x1, other arithmetic, per_device(): return current.astype(jnp.bfloat16)  11.3 us
    all_to_all x1, blocking collectives, per_device(): lax.all_to_all(pieces, 'member', split_axis=2, concat_axis=0, tiled=True)  11.2 us
  transfers between devices with their start and end apart: 2, of which 2 were waited for; matrix products, arithmetic and copies ran while one was open for 1% of the time, Pallas kernels for 0%

commit v1 on v0

v1 whole, which is shorter than its diff:
```python
import jax
import jax.numpy as jnp
from jax import lax
from jax.sharding import PartitionSpec as P

PLE = 256
epsilon = 1e-06


def norm_rows(values, scales):
    return values * lax.rsqrt(jnp.mean(values * values, axis=-1, keepdims=True) + epsilon) * scales


def per_device(
    hidden,
    token_slab,
    token_row,
    slab_owner,
    ple_table,
    norm_gains,
    w_gate,
    w_up,
    w_down,
    ple_gate,
    ple_proj,
):
    members = lax.axis_size("member")
    devices = lax.axis_size("group") * members
    tokens_here = token_row.shape[0]
    slots = max(2, (2 * tokens_here + devices - 1) // devices)
    me = lax.axis_index("member")

    gate_full = lax.all_gather(ple_gate[0].T, "member", axis=0, tiled=True)
    proj_full = lax.all_gather(ple_proj[0], "member", axis=0, tiled=True)

    normed = norm_rows(hidden.astype(jnp.float32), norm_gains[0, 0]).astype(jnp.bfloat16)
    gate_part = jnp.dot(normed, w_gate[0], preferred_element_type=jnp.float32)
    up_part = jnp.dot(normed, w_up[0], preferred_element_type=jnp.float32)
    activated = (jax.nn.gelu(gate_part, approximate=True) * up_part).astype(jnp.bfloat16)
    partial = jnp.dot(activated, w_down[0], preferred_element_type=jnp.float32).astype(jnp.bfloat16)
    mlp_out = lax.psum_scatter(partial, "member", scatter_dimension=0, tiled=True).astype(jnp.float32)

    target = slab_owner[token_slab[:, 0]]
    order = jnp.arange(tokens_here, dtype=jnp.int32)
    earlier = (target[None, :] == target[:, None]) & (order[None, :] < order[:, None])
    slot_of = jnp.sum(earlier.astype(jnp.int32), axis=1)
    hit_map = (target[:, None, None] == jnp.arange(devices, dtype=jnp.int32)[None, :, None]) & (
        slot_of[:, None, None] == jnp.arange(slots, dtype=jnp.int32)[None, None, :]
    )
    requests = jnp.sum(jnp.where(hit_map, token_row[:, None, None] + 1, 0), axis=0)
    received = lax.all_to_all(requests, ("group", "member"), split_axis=0, concat_axis=0, tiled=True)
    flat_ids = received.reshape(-1) - 1
    one_hot = (flat_ids[:, None] == jnp.arange(ple_table.shape[0], dtype=jnp.int32)[None, :]).astype(jnp.bfloat16)
    served = jnp.dot(one_hot, ple_table, preferred_element_type=jnp.float32).astype(jnp.bfloat16)
    served = served.reshape(devices, slots * ple_table.shape[1])
    returned = lax.all_to_all(served, ("group", "member"), split_axis=0, concat_axis=0, tiled=True)
    returned = returned.reshape(devices * slots, ple_table.shape[1])
    own_rows = jnp.dot(hit_map.reshape(tokens_here, devices * slots).astype(jnp.bfloat16), returned,
                       preferred_element_type=jnp.float32)

    mine = lax.dynamic_slice_in_dim(hidden, me * tokens_here, tokens_here, 0).astype(jnp.float32)
    current = mine + norm_rows(mlp_out, norm_gains[0, 1])
    current_b = current.astype(jnp.bfloat16)
    gate_out = lax.dot_general(current_b, gate_full, (((1,), (1,)), ((), ())), preferred_element_type=jnp.float32)
    ple_act = (jax.nn.gelu(gate_out, approximate=True) * (own_rows * PLE**0.5)).astype(jnp.bfloat16)
    ple_out = jnp.dot(ple_act, proj_full, preferred_element_type=jnp.float32)
    current = current + norm_rows(ple_out, norm_gains[0, 2])
    return lax.all_gather(current.astype(jnp.bfloat16), "member", axis=0, tiled=True)


def solution(mesh):
    return jax.shard_map(
        per_device,
        mesh=mesh,
        in_specs=(
            P("group", None),
            P(("group", "member"), None),
            P(("group", "member")),
            P(),
            P(("group", "member"), None),
            P(),
            P(None, None, "member"),
            P(None, None, "member"),
            P(None, "member", None),
            P(None, None, "member"),
            P(None, "member", None),
        ),
        out_specs=P("group", None),
        check_vma=False,
    )
```

time: 438 us -> 283 us (0.65)
  waiting for transfers between devices: 306 us -> 195 us
  blocking collectives: 51.9 us -> 20.7 us
  other arithmetic: 27 us -> 13 us
  matrix products: 32.3 us -> 25.3 us
  starting transfers between devices: 0.04 us -> 4.71 us
    psum x2 -> x0, waiting for transfers between devices: 306 us -> none  [combine_branch(): summed = lax.psum(partial_value, 'member')]
    all_gather x0 -> x3, waiting for transfers between devices: none -> 146 us  [the longest x1 60.6 us: per_device(): lax.all_gather(current.astype(jnp.bfloat16), 'member', axis=0, tiled=True)]
    reduce_scatter x0 -> x1, waiting for transfers between devices: none -> 37.6 us  [per_device(): lax.psum_scatter(partial, 'member', scatter_dimension=0, tiled=True)]
    all_to_all x4 -> x1, blocking collectives: 51.9 us -> 20.7 us  [per_device(): lax.all_to_all(requests, ('group', 'member'), split_axis=0, concat_axis=0...]
    all_to_all x0 -> x1, waiting for transfers between devices: none -> 10.7 us  [per_device(): lax.all_to_all(served, ('group', 'member'), split_axis=0, concat_axis=0,...]
    reduce_sum x3 -> x2, other arithmetic: 15.3 us -> 5.47 us  [norm_rows(): jnp.mean(values * values, axis=-1, keepdims=True) + epsilon]
    convert_element_type x1, other arithmetic: 11.3 us -> 2.1 us  [per_device(): current.astype(jnp.bfloat16)]
    dot_general x4, matrix products: 25.5 us -> 18.5 us  [the longest x1 12.4 us: per_device(): jnp.dot(activated, w_down[0], preferred_element_type=jnp.float32)]
  transfers between devices with their start and end apart: 2 -> 5, of which waited for: 2 -> 5; matrix products, arithmetic and copies ran while one was open for 1% -> 4% of each run, Pallas kernels for 0% -> 0%
where the time goes in v1:
time: 283 us; the launch traced here: 282 us
  waiting for transfers between devices  195 us (69%)
  matrix products  25.3 us (9%)
  blocking collectives  20.7 us (7%)
  between operations  13.3 us (5%)
  other arithmetic  13 us (5%)
  local copies, waits for them, and re-layouts  10 us (4%)
  starting transfers between devices  4.71 us (2%)
    all_gather x1, waiting for transfers between devices, per_device(): lax.all_gather(current.astype(jnp.bfloat16), 'member', axis=0, tiled=True)  60.6 us
    all_gather x1, waiting for transfers between devices, per_device(): gate_full = lax.all_gather(ple_gate[0].T, 'member', axis=0, tiled=True)  42.8 us
    all_gather x1, waiting for transfers between devices, per_device(): proj_full = lax.all_gather(ple_proj[0], 'member', axis=0, tiled=True)  42 us
    reduce_scatter x1, waiting for transfers between devices, per_device(): lax.psum_scatter(partial, 'member', scatter_dimension=0, tiled=True)  37.6 us
    all_to_all x1, blocking collectives, per_device(): lax.all_to_all(requests, ('group', 'member'), split_axis=0, concat_axis=0...  20.7 us
    dot_general x1, matrix products, per_device(): jnp.dot(activated, w_down[0], preferred_element_type=jnp.float32)  12.4 us
    all_to_all x1, waiting for transfers between devices, per_device(): lax.all_to_all(served, ('group', 'member'), split_axis=0, concat_axis=0,...  10.7 us
    unnamed x19, local copies, waits for them, and re-layouts  7.92 us
  transfers between devices with their start and end apart: 5, of which 5 were waited for; matrix products, arithmetic and copies ran while one was open for 4% of the time, Pallas kernels for 0%

profile of v1, /device:TPU:0, one launch (start us, length us, event | category | flops | bytes accessed | tf_op | source)
XLA Modules:
  0.0 282.3 jit_solution(1658720977791138758)
XLA Ops:
  6.5 4.2 %fusion = f32[1536]{0:T(1024)S(1)} fusion(bf16[1536,2048]{1,0:T(8,128)(2,1)} %param.11), kind=kLoop, calls=%fused_computation.3 | loop fusion | flops 9435648 | bytes 6297600 | tf_op jit(solution)/shard_map/reduce_sum | solution.py:11
  11.3 6.8 %fusion.13 = f32[1536,512]{1,0:T(8,128)} fusion(bf16[1,2048,512]{2,1,0:T(8,128)(2,1)} %param.17, bf16[1536,2048]{1,0:T(8,128)(2,1)S(1)} %copy-done.2, f32[2048]{0:T(1024)S(1)} %bitcast.36, f32[1536]{0:T(1024)S(1)} %add_rsqrt_fusion), kind=kOutput, calls=%fused_computation.19 | convolution fusion | flops 3233808384 | bytes 11548672 | tf_op jit(solution)/shard_map/dot_general | solution.py:37
  18.1 12.4 %convolution_convert_fusion = bf16[1536,2048]{1,0:T(8,128)(2,1)} fusion(bf16[1,512,2048]{2,1,0:T(8,128)(2,1)S(1)} %copy-done, f32[1536,512]{1,0:T(8,128)} %fusion.13, bf16[1,2048,512]{2,1,0:T(8,128)(2,1)} %param.18, bf16[1536,2048]{1,0:T(8,128)(2,1)} %param.11, f32[2048]{0:T(1024)S(1)} %bitcast.37, f32[1536]{0:T(1024)S(1)} %add_rsqrt_fusion), kind=kOutput, calls=%fused_computation.6 | convolution fusion | flops 6466043904 | bytes 19937280 | tf_op jit(solution)/shard_map/dot_general | solution.py:40
  30.6 0.7 all-gather.5.cloned.1.call-update
  31.3 0.7 all-gather.9.cloned.1.call-update
  32.1 1.2 gather_fusion
  33.5 2.2 select_reduce_fusion
  35.8 20.7 %all_to_all.19 = s32[128,1,2]{2,1,0:T(1,128)S(1)} all-to-all(s32[128,1,2]{2,1,0:T(1,128)S(1)} %bitcast.31), channel_id=1, replica_groups=mesh['group'=8,'member'=16] {'group','member'}, dimensions={0} | all-to-all | bytes 2048 | tf_op jit(solution)/shard_map/all_to_all | solution.py:51
  56.8 1.8 fusion.22
  59.2 1.4 reduce.5
  60.6 0.7 reshape.127
  61.3 4.6 %all-to-all-start.1 = ((bf16[128,2,256]{2,1,0:T(2,128)(2,1)}), bf16[128,2,256]{2,1,0:T(2,128)(2,1)S(1)}, u32[]{:S(2)}, u32[]{:S(2)}) async-start(bf16[128,2,256]{2,1,0:T(2,128)(2,1)} %reshape.127), calls=%async_computation.2 | async-start | bytes 262144 | tf_op jit(solution)/shard_map/all_to_all | solution.py:56
  66.0 10.7 %all-to-all-done.1 = bf16[128,2,256]{2,1,0:T(2,128)(2,1)S(1)} async-done(((bf16[128,2,256]{2,1,0:T(2,128)(2,1)}), bf16[128,2,256]{2,1,0:T(2,128)(2,1)S(1)}, u32[]{:S(2)}, u32[]{:S(2)}) %all-to-all-start.1) | async-done | bytes 131104 | tf_op jit(solution)/shard_map/all_to_all | solution.py:56
  76.8 0.8 reduce.1
  77.6 37.6 %reduce-scatter.2.cloned.1.call-done = bf16[96,2048]{1,0:T(8,128)(2,1)} async-done(((bf16[1536,2048]{1,0:T(8,128)(2,1)}), bf16[96,2048]{1,0:T(8,128)(2,1)}) %reduce-scatter.2.cloned.1.call-update) | async-done | bytes 393232 | tf_op jit(solution)/shard_map/reduce_scatter | solution.py:41
  115.2 1.2 fusion.28
  116.5 42.8 %all-gather.5.cloned.1.call-done = bf16[256,2048]{1,0:T(8,128)(2,1)} async-done(((bf16[16,2048]{1,0:T(8,128)(2,1)}), bf16[256,2048]{1,0:T(8,128)(2,1)}) %all-gather.5.cloned.1.call-update) | async-done | bytes 1048592 | tf_op jit(solution)/shard_map/all_gather | solution.py:33
  159.3 2.0 fusion.43
  161.3 42.0 %all-gather.9.cloned.1.call-done = bf16[1,256,2048]{2,1,0:T(8,128)(2,1)} async-done(((bf16[1,16,2048]{2,1,0:T(8,128)(2,1)}), bf16[1,256,2048]{2,1,0:T(8,128)(2,1)}) %all-gather.9.cloned.1.call-update) | async-done | bytes 1048592 | tf_op jit(solution)/shard_map/all_gather | solution.py:34
  203.4 2.3 multiply_reduce_fusion
  205.7 0.7 add_rsqrt_fusion.1
  206.4 2.1 add_convert_fusion
  208.5 60.6 %all-gather.7.cloned.1.call-done = bf16[1536,2048]{1,0:T(8,128)(2,1)} async-done(((bf16[96,2048]{1,0:T(8,128)(2,1)}), bf16[1536,2048]{1,0:T(8,128)(2,1)}) %all-gather.7.cloned.1.call-update) | async-done | bytes 6291472 | tf_op jit(solution)/shard_map/all_gather | solution.py:68
  269.1 6.6 %copy.17 = bf16[1536,2048]{1,0:T(8,128)(2,1)} copy(bf16[1536,2048]{1,0:T(8,128)(2,1)} %all-gather.7.cloned.1.call-done) | data formatting | bytes 12582912
  (38 shorter events, 2.1 us)
Async XLA Ops:
  6.5 11.6 %copy-start = (bf16[1,512,2048]{2,1,0:T(8,128)(2,1)S(1)}, bf16[1,512,2048]{2,1,0:T(8,128)(2,1)}, u32[]{:S(2)}) copy-start(bf16[1,512,2048]{2,1,0:T(8,128)(2,1)} %param.19) | copy-start | bytes 6291460
  6.5 4.3 %copy-start.4 = (f32[1,3,2048]{2,0,1:T(1,128)S(1)}, f32[1,3,2048]{2,0,1:T(1,128)}, u32[]{:S(2)}) copy-start(f32[1,3,2048]{2,0,1:T(1,128)} %param.16) | copy-start | bytes 73732
  6.5 108.7 %reduce-scatter.2.cloned.1.call-start = ((), (), s32[]{:S(2)}) async-start(), calls=%async_computation.3 | async-start | bytes 6684672 | tf_op jit(solution)/shard_map/reduce_scatter | solution.py:41
  6.5 4.8 %copy-start.2 = (bf16[1536,2048]{1,0:T(8,128)(2,1)S(1)}, bf16[1536,2048]{1,0:T(8,128)(2,1)}, u32[]{:S(2)}) copy-start(bf16[1536,2048]{1,0:T(8,128)(2,1)} %param.11) | copy-start | bytes 18874372
  30.5 1.5 copy-start.6
  30.5 1.5 copy-start.7
  30.5 1.6 copy-start.1
  30.5 128.8 %all-gather.5.cloned.1.call-start = ((), (), s32[]{:S(2)}) async-start(), calls=%async_computation.4 | async-start | bytes 1114112 | tf_op jit(solution)/shard_map/all_gather | solution.py:33
  31.3 172.1 %all-gather.9.cloned.1.call-start = ((), (), s32[]{:S(2)}) async-start(), calls=%async_computation.6 | async-start | bytes 1114112 | tf_op jit(solution)/shard_map/all_gather | solution.py:34
  61.3 15.4 %all-to-all-start.1 = ((bf16[128,2,256]{2,1,0:T(2,128)(2,1)}), bf16[128,2,256]{2,1,0:T(2,128)(2,1)S(1)}, u32[]{:S(2)}, u32[]{:S(2)}) async-start(bf16[128,2,256]{2,1,0:T(2,128)(2,1)} %reshape.127), calls=%async_computation.2 | async-start | bytes 262144 | tf_op jit(solution)/shard_map/all_to_all | solution.py:56
  65.9 203.3 %all-gather.7.cloned.1.call-start = ((), (), s32[]{:S(2)}) async-start(), calls=%async_computation.5 | async-start | bytes 6684672 | tf_op jit(solution)/shard_map/all_gather | solution.py:68
  115.2 91.1 %copy-start.3 = (bf16[96,2048]{1,0:T(8,128)(2,1)S(1)}, bf16[96,2048]{1,0:T(8,128)(2,1)}, u32[]{:S(2)}) copy-start(bf16[96,2048]{1,0:T(8,128)(2,1)} %reduce-scatter.2.cloned.1.call-done) | copy-start | bytes 1179652
  116.5 44.8 %copy-start.5 = (f32[96]{0:T(128)}, f32[96]{0:T(128)S(1)}, u32[]{:S(2)}) copy-start(f32[96]{0:T(128)S(1)} %add_rsqrt_fusion.2) | copy-start | bytes 1156
Sparse Core Ops, SparseCore 0:
  30.6 84.5 reduce-scatter.1
  117.4 41.9 all-gather.4
  161.5 41.8 all-gather.8
  208.6 60.4 all-gather.6

commit v2 on v1

v2 whole, which is shorter than its diff:
```python
import functools

import jax
import jax.numpy as jnp
from jax import lax
from jax.experimental import pallas as pl
from jax.experimental.pallas import tpu as pltpu
from jax.sharding import PartitionSpec as P

EPS = 1e-06
MESH = pl.DeviceIdType.MESH
BF, F32 = jnp.bfloat16, jnp.float32
SIDE = 4
GROUPS = (
    ((2, 2), (2, 1), (2, 3), (2, 0)),
    ((0, 2), (1, 2), (3, 2), (1, 1)),
    ((1, 3), (3, 1), (3, 3), (1, 0)),
    ((3, 0), (0, 1), (0, 3), (0, 0)),
)
ORDER = [piece for group in GROUPS for piece in group]


def slot(h, da, db):
    return ORDER.index((da, db) if h == 0 else (db, da))


def gelu(v):
    return 0.5 * v * (1.0 + jnp.tanh(0.7978845608028654 * (v + 0.044715 * (v * v * v))))


def rms_scale(v):
    return lax.rsqrt(jnp.mean(v * v, axis=-1, keepdims=True) + EPS)


def diagonal_column(row, n):
    eye = lax.broadcasted_iota(jnp.int32, (n, n), 0) == lax.broadcasted_iota(jnp.int32, (n, n), 1)
    return jnp.sum(jnp.where(eye, row, 0.0), axis=1, keepdims=True)


def body(
    nz, slab_rows,
    hid_hbm, wg_hbm, wu_hbm, wd_hbm, pg_hbm, pp_hbm, table_hbm, gains, slab, rowid, owner,
    out,
    hid, own, wg, wu, wd, table, act, part, r1a, r1b, r2a, r2b, ids, a0, a1, a2, a3, a4, wb,
    local_sem, ss1a, rs1a, ss1b, rs1b, ss2a, rs2a, ss2b, rs2b, sg1, rg1, sg2, rg2, sg3, rg3, sg4, rg4,
    sid, rid, sw, rw, sx, rx,
):
    tok, d = own.shape
    half, t2 = d // 2, tok // 2
    lanes = wb.shape[-1]
    pw = table.shape[1]
    ndev = nz * 2 * SIDE * SIDE
    g, m = lax.axis_index("group"), lax.axis_index("member")
    z, c = g // 2, lax.rem(g, 2)
    x, y = m // SIDE, lax.rem(m, SIDE)

    def at(dx, dy):
        return lax.rem(x + dx, SIDE) * SIDE + lax.rem(y + dy, SIDE)

    def along(axis, off):
        if axis == "x":
            return (g, at(off, 0))
        if axis == "y":
            return (g, at(0, off))
        if axis == "z":
            return (lax.rem(z + off, nz) * 2 + c, m)
        return (z * 2 + 1 - c, m)

    def send(src, dst, s, r, dev):
        copy = pltpu.make_async_remote_copy(
            src_ref=src, dst_ref=dst, send_sem=s, recv_sem=r, device_id=dev, device_id_type=MESH
        )
        return copy

    sizes = {"y": SIDE, "x": SIDE, "z": nz, "c": 2}
    peers = [(a, o) for a in "yxzc" for o in range(1, sizes[a])]

    locals_ = []

    def local(src, dst):
        copy = pltpu.make_async_copy(src, dst, local_sem.at[len(locals_)])
        copy.start()
        locals_.append(copy)
        return copy

    lane0 = pl.multiple_of(g * lanes, 128)
    hid_in = []
    in_pg = local(pg_hbm.at[:, pl.ds(lane0, lanes)], wb.at[z, c, 0, x, y])
    in_pp = local(pp_hbm.at[:, pl.ds(lane0, lanes)], wb.at[z, c, 1, x, y])
    for k, (dx, dy) in enumerate(ORDER):
        if k == 4:
            in_wg = local(wg_hbm, wg)
            in_wu = local(wu_hbm, wu)
            in_wd = local(wd_hbm, wd)
        hid_in.append(local(hid_hbm.at[at(dx, dy)], hid.at[k]))
    in_own = local(hid_hbm.at[m], own)
    in_table = local(table_hbm, table)

    barrier = pltpu.get_barrier_semaphore()
    for a, o in peers:
        pl.semaphore_signal(barrier, inc=1, device_id=along(a, o), device_id_type=MESH)

    owner_col = diagonal_column(owner[...].astype(F32), ndev)
    slab_row = slab[...]
    match = lax.broadcasted_iota(jnp.int32, (ndev, tok), 0) == slab_row
    target_row = jnp.sum(jnp.where(match, owner_col, 0.0), axis=0, keepdims=True)
    ids[z, c, x, y] = target_row * float(slab_rows) + rowid[...].astype(F32)

    pl.semaphore_wait(barrier, len(peers))

    started = []

    def exchange(ref_of, dst_of, s, r, axis, base):
        copies = []
        for o in range(1, sizes[axis]):
            n = base + o - 1
            copy = send(ref_of(o), dst_of(o), s.at[n], r.at[n], along(axis, o))
            copy.start()
            copies.append(copy)
        started.extend(copies)
        return copies

    base_of = {"y": 0, "x": SIDE - 1, "z": 2 * SIDE - 2, "c": 2 * SIDE - 3 + nz}

    def gather_stage(ref, with_t, s, r, axis):
        if axis == "y":
            view = ref.at[z, c, :, x, y] if with_t else ref.at[z, c, x, y]
        elif axis == "x":
            view = ref.at[z, c, :, x] if with_t else ref.at[z, c, x]
        elif axis == "z":
            view = ref.at[z, c]
        else:
            view = ref.at[:, c]
        return exchange(lambda o: view, lambda o: view, s, r, axis, base_of[axis])

    def arrive(copies):
        for copy in copies:
            copy.wait_recv()

    def gathers(axis):
        return gather_stage(ids, False, sid, rid, axis) + gather_stage(wb, True, sw, rw, axis)

    in_pg.wait()
    in_pp.wait()
    flight = gathers("y")

    m1a, m1b, m2a, m2b = {}, {}, {}, {}
    rows = (slice(0, t2), slice(t2, tok))
    first_axis, second_axis = ("x", "y"), ("y", "x")
    step = (1, SIDE - 1)

    def go(table_, key, src, dst, s, r, dev):
        copy = send(src, dst, s, r, dev)
        copy.start()
        table_[key] = copy
        started.append(copy)

    def send_1b(h, way, db, t):
        da = step[way]
        go(m1b, (h, way, db, t), part.at[h, slot(h, da, db), rows[t]], r1b.at[h, way, db, rows[t]],
           ss1b.at[h, way, db, t], rs1b.at[h, way, db, t], along(first_axis[h], step[way]))

    def send_ready(piece):
        for h in range(2):
            da, db = piece if h == 0 else piece[::-1]
            if da == 2:
                for way in range(2):
                    go(m1a, (h, way, db), part.at[h, slot(h, 2, db), rows[way]], r1a.at[h, way, db],
                       ss1a.at[h, way, db], rs1a.at[h, way, db], along(first_axis[h], step[way]))
            elif da == 1:
                send_1b(h, 0, db, 1)
            elif da == 3:
                send_1b(h, 1, db, 0)

    def compute(gi):
        k0 = gi * 4
        for k in range(k0, k0 + 4):
            hid_in[k].wait()
        gain = gains[0]

        @pl.loop(0, 4)
        def _(i):
            v = hid[k0 + i].astype(F32)
            hid[k0 + i] = (v * rms_scale(v) * gain).astype(BF)

        n = wg.shape[1]
        tile = min(256, n)
        if gi == 0:
            in_wg.wait()
            in_wu.wait()

        @pl.loop(0, n // tile)
        def _(j):
            cols = pl.ds(pl.multiple_of(j * tile, 128), tile)
            v = hid[k0:k0 + 4].reshape(4 * tok, d)
            gate = jnp.dot(v, wg[:, cols], preferred_element_type=F32)
            up = jnp.dot(v, wu[:, cols], preferred_element_type=F32)
            act[:, cols] = (gelu(gate) * up).astype(BF)

        if gi == 0:
            in_wd.wait()
        dt = min(256, half)
        per = half // dt

        @pl.loop(0, 2 * per)
        def _(j):
            cols = pl.ds(pl.multiple_of(j * dt, 128), dt)
            out_cols = pl.ds(pl.multiple_of(lax.rem(j, per) * dt, 128), dt)
            v = jnp.dot(act[...], wd[:, cols], preferred_element_type=F32).astype(BF)
            part[j // per, k0:k0 + 4, :, out_cols] = v.reshape(4, tok, dt)

        for piece in GROUPS[gi]:
            send_ready(piece)

    def add_into(h, k, r, other):
        part[h, k, r] = (part[h, k, r].astype(F32) + other[...].astype(F32)).astype(BF)

    def relay_1b(db):
        for h in range(2):
            for way in range(2):
                m1a[h, way, db].wait_recv()
                add_into(h, slot(h, step[way], db), rows[way], r1a.at[h, way, db])
                send_1b(h, way, db, way)

    compute(0)
    arrive(flight)
    flight = gathers("x")
    compute(1)
    arrive(flight)
    flight = gathers("z")
    compute(2)
    relay_1b(2)
    arrive(flight)
    flight = gathers("c")
    compute(3)
    for db in (1, 3, 0):
        relay_1b(db)
    arrive(flight)

    in_table.wait()
    rel = ids[...].reshape(ndev, tok) - ((g * SIDE * SIDE + m) * slab_rows).astype(F32)
    hit = (rel >= 0.0) & (rel < float(slab_rows))
    lane = lax.broadcasted_iota(jnp.int32, (ndev, tok), 1).astype(F32)
    first = jnp.min(jnp.where(hit, lane, 1e4), axis=1, keepdims=True)
    last = jnp.max(jnp.where(hit, lane, -1.0), axis=1, keepdims=True)
    id0 = jnp.sum(jnp.where(hit & (lane == first), rel, 0.0), axis=1, keepdims=True)
    id1 = jnp.sum(jnp.where(hit & (lane == last), rel, 0.0), axis=1, keepdims=True)
    id0 = jnp.where(first < 5e3, id0, -1.0).astype(jnp.int32)
    id1 = jnp.where(last > first, id1, -1.0).astype(jnp.int32)
    row_iota = lax.broadcasted_iota(jnp.int32, (ndev, slab_rows), 1)
    for i, wanted in enumerate((id0, id1)):
        pick = jnp.where(row_iota == wanted, 1.0, 0.0).astype(BF)
        served = jnp.dot(pick, table[...], preferred_element_type=F32)
        a0[:, :, :, :, :, i * pw:(i + 1) * pw] = served.reshape(nz, 2, SIDE, SIDE, 1, pw)

    def return_c():
        a1[:, c] = a0[:, c]
        return exchange(lambda o: a0.at[:, 1 - c], lambda o: a1.at[:, c], sx, rx, "c", base_of["c"])

    def return_z():
        a2[z] = a1[z]
        return exchange(lambda o: a1.at[lax.rem(z + o, nz)], lambda o: a2.at[z], sx, rx, "z", base_of["z"])

    def return_x():
        a3[:, :, x] = a2[:, :, x]
        return exchange(
            lambda o: a2.at[:, :, lax.rem(x + o, SIDE)], lambda o: a3.at[:, :, x], sx, rx, "x", base_of["x"])

    def return_y():
        a4[:, :, :, y] = a3[:, :, :, y]
        return exchange(
            lambda o: a3.at[:, :, :, lax.rem(y + o, SIDE)], lambda o: a4.at[:, :, :, y], sx, rx, "y", base_of["y"])

    def sum_first(db):
        for h in range(2):
            for way in range(2):
                for t in range(2):
                    m1b[h, way, db, t].wait_recv()
            k = slot(h, 0, db)
            total = part[h, k].astype(F32) + r1b[h, 0, db].astype(F32) + r1b[h, 1, db].astype(F32)
            part[h, k] = total.astype(BF)
            if db == 2:
                for way in range(2):
                    go(m2a, (h, way), part.at[h, k, rows[way]], r2a.at[h, way],
                       ss2a.at[h, way], rs2a.at[h, way], along(second_axis[h], step[way]))
            elif db == 1:
                send_2b(h, 0, 1)
            elif db == 3:
                send_2b(h, 1, 0)

    def send_2b(h, way, t):
        go(m2b, (h, way, t), part.at[h, slot(h, 0, step[way]), rows[t]], r2b.at[h, way, rows[t]],
           ss2b.at[h, way, t], rs2b.at[h, way, t], along(second_axis[h], step[way]))

    flight = return_c()
    sum_first(2)
    arrive(flight)
    flight = return_z()
    sum_first(1)
    arrive(flight)
    flight = return_x()
    sum_first(3)
    for h in range(2):
        for way in range(2):
            m2a[h, way].wait_recv()
            add_into(h, slot(h, 0, step[way]), rows[way], r2a.at[h, way])
            send_2b(h, way, way)
    arrive(flight)
    flight = return_y()
    sum_first(0)
    for h in range(2):
        for way in range(2):
            for t in range(2):
                m2b[h, way, t].wait_recv()

    in_own.wait()
    sums = [
        part[h, slot(h, 0, 0)].astype(F32) + r2b[h, 0].astype(F32) + r2b[h, 1].astype(F32) for h in range(2)
    ]
    mlp = jnp.concatenate(sums, axis=1)
    current = own[...].astype(F32) + mlp * rms_scale(mlp) * gains[1]
    current_b = current.astype(BF)
    nb = nz * 2
    gate = jnp.zeros((tok, SIDE * SIDE * wb.shape[5]), F32)
    for b in range(nb):
        w = wb[b // 2, b % 2, 0].reshape(SIDE * SIDE * wb.shape[5], lanes)
        gate += lax.dot_general(
            current_b[:, b * lanes:(b + 1) * lanes], w, (((1,), (1,)), ((), ())), preferred_element_type=F32)

    arrive(flight)
    target_col = diagonal_column(target_row, tok)
    i0 = lax.broadcasted_iota(jnp.int32, (tok, tok), 0)
    i1 = lax.broadcasted_iota(jnp.int32, (tok, tok), 1)
    second = jnp.max(jnp.where((target_col == target_row) & (i1 < i0), 1.0, 0.0), axis=1, keepdims=True)
    owners = lax.broadcasted_iota(jnp.int32, (tok, ndev), 1).astype(F32) == target_col
    looked = jnp.zeros((tok, pw), F32)
    for i in range(2):
        pick = jnp.where(owners & (second == float(i)), 1.0, 0.0).astype(BF)
        rows_i = a4[:, :, :, :, :, i * pw:(i + 1) * pw].reshape(ndev, pw).astype(BF)
        looked += jnp.dot(pick, rows_i, preferred_element_type=F32)
    ple_act = (gelu(gate) * (looked * float(pw) ** 0.5)).astype(BF)
    ple = jnp.concatenate(
        [
            jnp.dot(ple_act, wb[b // 2, b % 2, 1].reshape(SIDE * SIDE * wb.shape[5], lanes),
                    preferred_element_type=F32)
            for b in range(nb)
        ],
        axis=1,
    )
    out[m] = (current + ple * rms_scale(ple) * gains[2]).astype(BF)

    cols = (slice(0, half), slice(half, d))
    g1, g2, g3, g4 = {}, {}, {}, {}

    def member(h, da, db):
        return at(da, db) if h == 0 else at(db, da)

    def spread(h, db):
        for way in range(2):
            view = out.at[member(h, 0, db), :, cols[h]]
            go(g3, (h, way, db), view, view, sg3.at[h, way, db], rg3.at[h, way, db],
               along(first_axis[h], step[way]))

    for h in range(2):
        for way in range(2):
            view = out.at[m, :, cols[h]]
            go(g1, (h, way), view, view, sg1.at[h, way], rg1.at[h, way], along(second_axis[h], step[way]))
    for h in range(2):
        spread(h, 0)
    for way in range(2):
        for h in range(2):
            g1[h, way].wait_recv()
            view = out.at[member(h, 0, step[1 - way]), rows[way], cols[h]]
            go(g2, (h, way), view, view, sg2.at[h, way], rg2.at[h, way], along(second_axis[h], step[way]))
    for db in (1, 3):
        for h in range(2):
            spread(h, db)

    def forward(db):
        for h in range(2):
            for way in range(2):
                g3[h, way, db].wait_recv()
                view = out.at[member(h, step[1 - way], db), rows[way], cols[h]]
                go(g4, (h, way, db), view, view, sg4.at[h, way, db], rg4.at[h, way, db],
                   along(first_axis[h], step[way]))

    for h in range(2):
        for way in range(2):
            g2[h, way].wait_recv()
        spread(h, 2)
    for db in (0, 1, 3, 2):
        forward(db)
    for copy in g4.values():
        copy.wait_recv()
    for copy in started:
        copy.wait_send()


def per_device(
    hidden, token_slab, token_row, slab_owner, ple_table, norm_gains, w_gate, w_up, w_down, ple_gate, ple_proj
):
    members = lax.axis_size("member")
    nz = lax.axis_size("group") // 2
    tok = token_row.shape[0]
    d, n = w_gate.shape[1:]
    slab_rows, pw = ple_table.shape
    half, t2 = d // 2, tok // 2
    per = ple_gate.shape[2]
    lanes = d // (2 * nz)
    dma = pltpu.SemaphoreType.DMA
    anyspace, vmem = pl.BlockSpec(memory_space=pl.ANY), pl.BlockSpec(memory_space=pltpu.VMEM)
    stages = 2 * (SIDE - 1) + nz
    rows_buf = pltpu.VMEM((nz, 2, SIDE, SIDE, 1, 2 * pw), F32)
    pairs = [(2, 2, 4), (2, 2, 4, 2), (2, 2), (2, 2, 2), (2, 2), (2, 2), (2, 2, 4), (2, 2, 4), (stages,), (stages,), (stages,)]
    call = pl.pallas_call(
        functools.partial(body, nz, slab_rows),
        out_shape=jax.ShapeDtypeStruct((members, tok, d), BF),
        in_specs=[anyspace] * 7 + [vmem] * 4,
        out_specs=vmem,
        scratch_shapes=[
            pltpu.VMEM((16, tok, d), BF),
            pltpu.VMEM((tok, d), BF),
            pltpu.VMEM((d, n), BF),
            pltpu.VMEM((d, n), BF),
            pltpu.VMEM((n, d), BF),
            pltpu.VMEM((slab_rows, pw), BF),
            pltpu.VMEM((4 * tok, n), BF),
            pltpu.VMEM((2, 16, tok, half), BF),
            pltpu.VMEM((2, 2, 4, t2, half), BF),
            pltpu.VMEM((2, 2, 4, tok, half), BF),
            pltpu.VMEM((2, 2, t2, half), BF),
            pltpu.VMEM((2, 2, tok, half), BF),
            pltpu.VMEM((nz, 2, SIDE, SIDE, 1, tok), F32),
            rows_buf, rows_buf, rows_buf, rows_buf, rows_buf,
            pltpu.VMEM((nz, 2, 2, SIDE, SIDE, per, lanes), BF),
            dma((24,)),
        ] + [dma(shape) for shape in pairs for _ in range(2)],
        compiler_params=pltpu.CompilerParams(
            collective_id=0, has_side_effects=True, vmem_limit_bytes=60 * 1024 * 1024
        ),
        name="layer",
    )
    out = call(
        hidden.reshape(members, tok, d), w_gate[0], w_up[0], w_down[0], ple_gate[0].T, ple_proj[0], ple_table,
        norm_gains.reshape(3, 1, d), token_slab.reshape(1, tok), token_row.reshape(1, tok),
        slab_owner.reshape(1, -1),
    )
    return out.reshape(members * tok, d)


def solution(mesh):
    return jax.shard_map(
        per_device,
        mesh=mesh,
        in_specs=(
            P("group", None),
            P(("group", "member"), None),
            P(("group", "member")),
            P(),
            P(("group", "member"), None),
            P(),
            P(None, None, "member"),
            P(None, None, "member"),
            P(None, "member", None),
            P(None, None, "member"),
            P(None, "member", None),
        ),
        out_specs=P("group", None),
        check_vma=False,
    )
```

time: 283 us -> 108 us (0.38)
  waiting for transfers between devices: 195 us -> 0 us
  Pallas kernels: 0 us -> 101 us
  matrix products: 25.3 us -> 0 us
  blocking collectives: 20.7 us -> 0 us
  between operations: 13.3 us -> 0.01 us
  other arithmetic: 13 us -> 0 us
  starting transfers between devices: 4.71 us -> 0 us
  local copies, waits for them, and re-layouts: 10 us -> 6.61 us
    all_gather x3 -> x0, waiting for transfers between devices: 146 us -> none  [the longest x1 60.6 us: per_device(): lax.all_gather(current.astype(jnp.bfloat16), 'member', axis=0, tiled=True)]
    pallas_call x0 -> x1, Pallas kernels: none -> 101 us  [per_device(): call(hidden.reshape(members, tok, d), w_gate[0], w_up[0], w_down[0], ple_...]
    reduce_scatter x1 -> x0, waiting for transfers between devices: 37.6 us -> none  [per_device(): lax.psum_scatter(partial, 'member', scatter_dimension=0, tiled=True)]
    dot_general x5 -> x0, matrix products: 25.3 us -> none  [the longest x1 12.4 us: per_device(): jnp.dot(activated, w_down[0], preferred_element_type=jnp.float32)]
    all_to_all x1 -> x0, blocking collectives: 20.7 us -> none  [per_device(): lax.all_to_all(requests, ('group', 'member'), split_axis=0, concat_axis=0...]
    all_to_all x1 -> x0, waiting for transfers between devices: 10.7 us -> none  [per_device(): lax.all_to_all(served, ('group', 'member'), split_axis=0, concat_axis=0,...]
    reduce_sum x4 -> x0, other arithmetic: 7.88 us -> none  [the longest x2 5.47 us: norm_rows(): jnp.mean(values * values, axis=-1, keepdims=True) + epsilon]
    all_to_all x1 -> x0, starting transfers between devices: 4.59 us -> none  [per_device(): lax.all_to_all(served, ('group', 'member'), split_axis=0, concat_axis=0,...]
  transfers between devices with their start and end apart: 5 -> 0, of which waited for: 5 -> 0; matrix products, arithmetic and copies ran while one was open for 4% -> 0% of each run, Pallas kernels for 0% -> 0%
where the time goes in v2:
time: 108 us
  Pallas kernels  101 us (94%)
  local copies, waits for them, and re-layouts  6.61 us (6%)
    pallas_call x1, Pallas kernels, per_device(): call(hidden.reshape(members, tok, d), w_gate[0], w_up[0], w_down[0], ple_...  101 us
    unnamed x1, local copies, waits for them, and re-layouts  6.61 us

profile of v2, /device:TPU:0, one launch (start us, length us, event | category | flops | bytes accessed | tf_op | source)
XLA Modules:
  0.0 107.8 jit_solution(8996562881162032519)
XLA Ops:
  0.0 101.2 %layer.1 = bf16[16,96,2048]{2,1,0:T(8,128)(2,1)} custom-call(bf16[16,96,2048]{2,1,0:T(8,128)(2,1)} %bitcast.14, bf16[2048,512]{1,0:T(8,128)(2,1)} %bitcast.15, bf16[2048,512]{1,0:T(8,128)(2,1)} %bitcast.16, bf16[512,2048]{1,0:T(8,128)(2,1)} %bitcast.17, bf16[16,2048]{1,0:T(8,128)(2,1)} %bitcast.18, bf16[16,2048]{1,0:T(8,128)(2,1)} %bitcast.19, ...), custom_call_target="tpu_custom_call" | custom-call | tf_op jit(solution)/shard_map/layer/pallas_call | solution.py:443
  101.2 6.6 %copy.13 = bf16[1536,2048]{1,0:T(8,128)(2,1)} copy(bf16[1536,2048]{1,0:T(8,128)(2,1)} %bitcast.13) | data formatting | bytes 12582912

commit v3 on v1

v3 whole, which is shorter than its diff:
```python
import functools

import jax
import jax.numpy as jnp
from jax import lax
from jax.experimental import pallas as pl
from jax.experimental.pallas import tpu as pltpu
from jax.sharding import PartitionSpec as P

EPS = 1e-06
MESH = pl.DeviceIdType.MESH
BF, F32 = jnp.bfloat16, jnp.float32
SIDE = 4
ORDER = [
    (2, 2), (1, 2), (2, 1), (3, 2), (2, 3),
    (1, 1), (1, 3), (3, 1), (3, 3), (0, 2), (2, 0),
    (0, 1), (1, 0), (0, 3), (3, 0), (0, 0),
]
SPLITS = ((0, 5, 11, 16), (0, 8, 16))
WAVES = (2, 1, 3, 0)


def slot(h, da, db):
    return ORDER.index((da, db) if h == 0 else (db, da))


def gelu(v):
    return 0.5 * v * (1.0 + jnp.tanh(0.7978845608028654 * (v + 0.044715 * (v * v * v))))


def rms_scale(v):
    return lax.rsqrt(jnp.mean(v * v, axis=-1, keepdims=True) + EPS)


def diagonal_column(row, n):
    eye = lax.broadcasted_iota(jnp.int32, (n, n), 0) == lax.broadcasted_iota(jnp.int32, (n, n), 1)
    return jnp.sum(jnp.where(eye, row, 0.0), axis=1, keepdims=True)


def body(
    nz, slab_rows,
    hid_hbm, wg_hbm, wu_hbm, wd_hbm, pg_hbm, pp_hbm, table_hbm, gains_hbm, slab_hbm, rowid_hbm, owner_hbm,
    out,
    hid, own, wg, wu, wd, table, act, part, r1a, r1b, r2a, r2b, ids, a0, a1, a2, a3, a4, wb,
    gains, slab, rowid, owner, looked,
    local_sem, ss1a, rs1a, ss1b, rs1b, ss2a, rs2a, ss2b, rs2b, sg1, rg1, sg2, rg2, sg3, rg3, sg4, rg4,
    sid, rid, sw, rw, sx, rx,
):
    tok, d = own.shape
    half, tq = d // 2, tok // 2
    quarter = half // 2
    lanes = wb.shape[-1]
    pw = table.shape[1]
    ndev = nz * 2 * SIDE * SIDE
    g, m = lax.axis_index("group"), lax.axis_index("member")
    z, c = g // 2, lax.rem(g, 2)
    x, y = m // SIDE, lax.rem(m, SIDE)
    toks = (slice(0, tq), slice(tq, tok))
    sub = (slice(0, quarter), slice(quarter, half))
    first_axis, second_axis = ("x", "y"), ("y", "x")
    step = (1, SIDE - 1)

    def at(dx, dy):
        return lax.rem(x + dx, SIDE) * SIDE + lax.rem(y + dy, SIDE)

    def along(axis, off):
        if axis == "x":
            return (g, at(off, 0))
        if axis == "y":
            return (g, at(0, off))
        if axis == "z":
            return (lax.rem(z + off, nz) * 2 + c, m)
        return (z * 2 + 1 - c, m)

    sizes = {"y": SIDE, "x": SIDE, "z": nz, "c": 2}
    peers = [(a, o) for a in "yxzc" for o in range(1, sizes[a])]

    barrier = pltpu.get_barrier_semaphore()
    for a, o in peers:
        pl.semaphore_signal(barrier, inc=1, device_id=along(a, o), device_id_type=MESH)

    locals_ = []

    def local(src, dst):
        copy = pltpu.make_async_copy(src, dst, local_sem.at[len(locals_)])
        copy.start()
        locals_.append(copy)
        return copy

    in_small = [local(owner_hbm, owner), local(slab_hbm, slab), local(rowid_hbm, rowid)]
    in_gains = local(gains_hbm, gains)
    hid_in = {}

    def load_hidden(q, k0, k1):
        for k in range(k0, k1):
            hid_in[q, k] = local(hid_hbm.at[at(*ORDER[k]), toks[q]], hid.at[q, k])

    load_hidden(0, 0, 5)
    lane0 = pl.multiple_of(g * lanes, 128)
    in_w = [
        local(pg_hbm.at[:, pl.ds(lane0, lanes)], wb.at[z, c, 0, x, y]),
        local(pp_hbm.at[:, pl.ds(lane0, lanes)], wb.at[z, c, 1, x, y]),
    ]
    in_wg = local(wg_hbm, wg)
    in_wu = local(wu_hbm, wu)
    in_wd = local(wd_hbm, wd)
    load_hidden(0, 5, 16)
    load_hidden(1, 0, 16)
    in_table = local(table_hbm, table)
    in_own = local(hid_hbm.at[m], own)

    for copy in in_small:
        copy.wait()
    owner_col = diagonal_column(owner[...].astype(F32), ndev)
    match = lax.broadcasted_iota(jnp.int32, (ndev, tok), 0) == slab[...]
    target_row = jnp.sum(jnp.where(match, owner_col, 0.0), axis=0, keepdims=True)
    ids[z, c, x, y] = target_row * float(slab_rows) + rowid[...].astype(F32)

    pl.semaphore_wait(barrier, len(peers))

    started = []

    def launch(src, dst, s, r, dev):
        copy = pltpu.make_async_remote_copy(
            src_ref=src, dst_ref=dst, send_sem=s, recv_sem=r, device_id=dev, device_id_type=MESH
        )
        copy.start()
        started.append(copy)
        return copy

    base = {"y": 0, "x": SIDE - 1, "z": 2 * SIDE - 2, "c": 2 * SIDE - 3 + nz}

    def exchange(ref_of, dst, s, r, axis):
        return [
            launch(ref_of(o), dst, s.at[base[axis] + o - 1], r.at[base[axis] + o - 1], along(axis, o))
            for o in range(1, sizes[axis])
        ]

    def arrive(copies):
        for copy in copies:
            copy.wait_recv()

    def gather_ids(axis):
        view = {"y": lambda: ids.at[z, c, x, y], "x": lambda: ids.at[z, c, x], "z": lambda: ids.at[z, c],
                "c": lambda: ids.at[:, c]}[axis]()
        return exchange(lambda o: view, view, sid, rid, axis)

    def gather_w(axis):
        view = {"y": lambda: wb.at[z, c, :, x, y], "x": lambda: wb.at[z, c, :, x], "z": lambda: wb.at[z, c],
                "c": lambda: wb.at[:, c]}[axis]()
        return exchange(lambda o: view, view, sw, rw, axis)

    m1a, m1b, m2a, m2b = {}, {}, {}, {}

    def send_1a(h, q, way, db):
        m1a[h, q, way, db] = launch(
            part.at[h, q, slot(h, 2, db), :, sub[way]], r1a.at[h, q, way, db],
            ss1a.at[h, q, way, db], rs1a.at[h, q, way, db], along(first_axis[h], step[way]))

    def send_1b(h, q, way, db, t):
        m1b[h, q, way, db, t] = launch(
            part.at[h, q, slot(h, step[way], db), :, sub[t]], r1b.at[h, q, way, db, :, sub[t]],
            ss1b.at[h, q, way, db, t], rs1b.at[h, q, way, db, t], along(first_axis[h], step[way]))

    def send_2a(h, q, way):
        m2a[h, q, way] = launch(
            part.at[h, q, slot(h, 0, 2), :, sub[way]], r2a.at[h, q, way],
            ss2a.at[h, q, way], rs2a.at[h, q, way], along(second_axis[h], step[way]))

    def send_2b(h, q, way, t):
        m2b[h, q, way, t] = launch(
            part.at[h, q, slot(h, 0, step[way]), :, sub[t]], r2b.at[h, q, way, :, sub[t]],
            ss2b.at[h, q, way, t], rs2b.at[h, q, way, t], along(second_axis[h], step[way]))

    def send_ready(q, i):
        todo = sorted(
            (WAVES.index(db), h, da, db)
            for h in range(2)
            for da, db in (p if h == 0 else p[::-1] for p in ORDER[SPLITS[q][i]:SPLITS[q][i + 1]])
        )
        for _, h, da, db in todo:
            if da == 2:
                for way in range(2):
                    send_1a(h, q, way, db)
        for _, h, da, db in todo:
            if da in (1, 3):
                way = step.index(da)
                send_1b(h, q, way, db, 1 - way)

    def compute(q, i, between=lambda: None):
        k0, k1 = SPLITS[q][i], SPLITS[q][i + 1]
        rows = (k1 - k0) * tq
        for k in range(k0, k1):
            hid_in[q, k].wait()
        if (q, i) == (0, 0):
            in_gains.wait()
        gain = gains[0]

        @pl.loop(0, k1 - k0)
        def _(k):
            v = hid[q, k0 + k].astype(F32)
            hid[q, k0 + k] = (v * rms_scale(v) * gain).astype(BF)

        n = wg.shape[1]
        tile = min(256, n)
        if (q, i) == (0, 0):
            in_wg.wait()
            in_wu.wait()

        @pl.loop(0, n // tile)
        def _(j):
            cols = pl.ds(pl.multiple_of(j * tile, 128), tile)
            v = hid[q, k0:k1].reshape(rows, d)
            gate = jnp.dot(v, wg[:, cols], preferred_element_type=F32)
            up = jnp.dot(v, wu[:, cols], preferred_element_type=F32)
            act[0:rows, cols] = (gelu(gate) * up).astype(BF)

        between()
        if (q, i) == (0, 0):
            in_wd.wait()
        dt = min(256, half)
        per = half // dt

        @pl.loop(0, 2 * per)
        def _(j):
            cols = pl.ds(pl.multiple_of(j * dt, 128), dt)
            out_cols = pl.ds(pl.multiple_of(lax.rem(j, per) * dt, 128), dt)
            v = jnp.dot(act[0:rows, :], wd[:, cols], preferred_element_type=F32).astype(BF)
            part[j // per, q, k0:k1, :, out_cols] = v.reshape(k1 - k0, tq, dt)

    def add_into(h, q, k, t, other):
        part[h, q, k, :, sub[t]] = (part[h, q, k, :, sub[t]].astype(F32) + other[...].astype(F32)).astype(BF)

    def relay_1(q, db):
        for h in range(2):
            for way in range(2):
                m1a[h, q, way, db].wait_recv()
                add_into(h, q, slot(h, step[way], db), way, r1a.at[h, q, way, db])
                send_1b(h, q, way, db, way)

    def sum_1(q, db):
        for h in range(2):
            for way in range(2):
                for t in range(2):
                    m1b[h, q, way, db, t].wait_recv()
            k = slot(h, 0, db)
            total = part[h, q, k].astype(F32) + r1b[h, q, 0, db].astype(F32) + r1b[h, q, 1, db].astype(F32)
            part[h, q, k] = total.astype(BF)
            if db == 2:
                for way in range(2):
                    send_2a(h, q, way)
            elif db in (1, 3):
                way = step.index(db)
                send_2b(h, q, way, 1 - way)

    def relay_2(q):
        for h in range(2):
            for way in range(2):
                m2a[h, q, way].wait_recv()
                add_into(h, q, slot(h, 0, step[way]), way, r2a.at[h, q, way])
                send_2b(h, q, way, way)

    def serve():
        in_table.wait()
        rel = ids[...].reshape(ndev, tok) - ((g * SIDE * SIDE + m) * slab_rows).astype(F32)
        hit = (rel >= 0.0) & (rel < float(slab_rows))
        lane = lax.broadcasted_iota(jnp.int32, (ndev, tok), 1).astype(F32)
        first = jnp.min(jnp.where(hit, lane, 1e4), axis=1, keepdims=True)
        last = jnp.max(jnp.where(hit, lane, -1.0), axis=1, keepdims=True)
        id0 = jnp.sum(jnp.where(hit & (lane == first), rel, 0.0), axis=1, keepdims=True)
        id1 = jnp.sum(jnp.where(hit & (lane == last), rel, 0.0), axis=1, keepdims=True)
        id0 = jnp.where(first < 5e3, id0, -1.0).astype(jnp.int32)
        id1 = jnp.where(last > first, id1, -1.0).astype(jnp.int32)
        row_iota = lax.broadcasted_iota(jnp.int32, (ndev, slab_rows), 1)
        for i, wanted in enumerate((id0, id1)):
            pick = jnp.where(row_iota == wanted, 1.0, 0.0).astype(BF)
            served = jnp.dot(pick, table[...], preferred_element_type=F32)
            a0[:, :, :, :, :, i * pw:(i + 1) * pw] = served.reshape(nz, 2, SIDE, SIDE, 1, pw)

    def return_c():
        a1[:, c] = a0[:, c]
        return exchange(lambda o: a0.at[:, 1 - c], a1.at[:, c], sx, rx, "c")

    def return_z():
        a2[z] = a1[z]
        return exchange(lambda o: a1.at[lax.rem(z + o, nz)], a2.at[z], sx, rx, "z")

    def return_x():
        a3[:, :, x] = a2[:, :, x]
        return exchange(lambda o: a2.at[:, :, lax.rem(x + o, SIDE)], a3.at[:, :, x], sx, rx, "x")

    def return_y():
        a4[:, :, :, y] = a3[:, :, :, y]
        return exchange(lambda o: a3.at[:, :, :, lax.rem(y + o, SIDE)], a4.at[:, :, :, y], sx, rx, "y")

    def look():
        target_col = diagonal_column(target_row, tok)
        i0 = lax.broadcasted_iota(jnp.int32, (tok, tok), 0)
        i1 = lax.broadcasted_iota(jnp.int32, (tok, tok), 1)
        second = jnp.max(jnp.where((target_col == target_row) & (i1 < i0), 1.0, 0.0), axis=1, keepdims=True)
        owners = lax.broadcasted_iota(jnp.int32, (tok, ndev), 1).astype(F32) == target_col
        rows = jnp.zeros((tok, pw), F32)
        for i in range(2):
            pick = jnp.where(owners & (second == float(i)), 1.0, 0.0).astype(BF)
            rows_i = a4[:, :, :, :, :, i * pw:(i + 1) * pw].reshape(ndev, pw).astype(BF)
            rows += jnp.dot(pick, rows_i, preferred_element_type=F32)
        looked[...] = rows * float(pw) ** 0.5

    nb = nz * 2
    channels = SIDE * SIDE * wb.shape[5]

    def finish(q):
        for h in range(2):
            for way in range(2):
                for t in range(2):
                    m2b[h, q, way, t].wait_recv()
        sums = [
            part[h, q, slot(h, 0, 0)].astype(F32) + r2b[h, q, 0].astype(F32) + r2b[h, q, 1].astype(F32)
            for h in range(2)
        ]
        mlp = jnp.concatenate(sums, axis=1)
        current = own[toks[q]].astype(F32) + mlp * rms_scale(mlp) * gains[1]
        current_b = current.astype(BF)
        gate = jnp.zeros((tq, channels), F32)
        for b in range(nb):
            w = wb[b // 2, b % 2, 0].reshape(channels, lanes)
            gate += lax.dot_general(
                current_b[:, b * lanes:(b + 1) * lanes], w, (((1,), (1,)), ((), ())), preferred_element_type=F32)
        ple_act = (gelu(gate) * looked[toks[q]]).astype(BF)
        ple = jnp.concatenate(
            [
                jnp.dot(ple_act, wb[b // 2, b % 2, 1].reshape(channels, lanes), preferred_element_type=F32)
                for b in range(nb)
            ],
            axis=1,
        )
        out[m, toks[q]] = (current + ple * rms_scale(ple) * gains[2]).astype(BF)

    g1, g2, g3, g4 = {}, {}, {}, {}

    def piece(h, q, da, db, t=None):
        lo = h * half + (0 if t is None else t * quarter)
        width = half if t is None else quarter
        return out.at[at(da, db) if h == 0 else at(db, da), toks[q], lo:lo + width]

    def publish(q):
        for h in range(2):
            for way in range(2):
                view = piece(h, q, 0, 0)
                g1[h, q, way] = launch(view, view, sg1.at[h, q, way], rg1.at[h, q, way],
                                       along(second_axis[h], step[way]))

    def spread(q, db):
        for h in range(2):
            for way in range(2):
                view = piece(h, q, 0, db)
                g3[h, q, way, db] = launch(view, view, sg3.at[h, q, way, db], rg3.at[h, q, way, db],
                                           along(first_axis[h], step[way]))

    def pass_on(q):
        for way in range(2):
            for h in range(2):
                g1[h, q, way].wait_recv()
                view = piece(h, q, 0, step[1 - way], way)
                g2[h, q, way] = launch(view, view, sg2.at[h, q, way], rg2.at[h, q, way],
                                       along(second_axis[h], step[way]))

    def settle(q):
        for h in range(2):
            for way in range(2):
                g2[h, q, way].wait_recv()

    def forward(q, db):
        for h in range(2):
            for way in range(2):
                g3[h, q, way, db].wait_recv()
                view = piece(h, q, step[1 - way], db, way)
                g4[h, q, way, db] = launch(view, view, sg4.at[h, q, way, db], rg4.at[h, q, way, db],
                                           along(first_axis[h], step[way]))

    fi = gather_ids("y")
    for copy in in_w:
        copy.wait()
    fw = gather_w("y")
    box = {}

    def early():
        arrive(fi)
        box["i"] = gather_ids("x")
        arrive(fw)
        box["w"] = gather_w("x")

    compute(0, 0, early)
    send_ready(0, 0)
    compute(0, 1)
    send_ready(0, 1)
    relay_1(0, 2)
    arrive(box["i"])
    fi = gather_ids("z")
    arrive(box["w"])
    fw = gather_w("z")
    compute(0, 2)
    send_ready(0, 2)
    relay_1(0, 1)
    relay_1(0, 3)
    relay_1(0, 0)
    arrive(fi)
    fi = gather_ids("c")
    compute(1, 0)
    sum_1(0, 2)
    send_ready(1, 0)
    arrive(fi)
    serve()
    fx = return_c()
    compute(1, 1)
    sum_1(0, 1)
    sum_1(0, 3)
    arrive(fx)
    fx = return_z()
    relay_2(0)
    send_ready(1, 1)
    relay_1(1, 2)
    arrive(fx)
    fx = return_x()
    relay_1(1, 1)
    relay_1(1, 3)
    relay_1(1, 0)
    arrive(fw)
    fw = gather_w("c")
    sum_1(0, 0)
    arrive(fx)
    fx = return_y()
    sum_1(1, 2)
    arrive(fx)
    in_own.wait()
    look()
    arrive(fw)
    finish(0)
    publish(0)
    spread(0, 0)
    sum_1(1, 1)
    sum_1(1, 3)
    relay_2(1)
    pass_on(0)
    spread(0, 1)
    spread(0, 3)
    sum_1(1, 0)
    settle(0)
    spread(0, 2)
    finish(1)
    publish(1)
    spread(1, 0)
    forward(0, 0)
    pass_on(1)
    spread(1, 1)
    spread(1, 3)
    forward(0, 1)
    forward(0, 3)
    settle(1)
    spread(1, 2)
    forward(0, 2)
    for db in (0, 1, 3, 2):
        forward(1, db)
    arrive(g4.values())
    for copy in started:
        copy.wait_send()


def per_device(
    hidden, token_slab, token_row, slab_owner, ple_table, norm_gains, w_gate, w_up, w_down, ple_gate, ple_proj
):
    members = lax.axis_size("member")
    nz = lax.axis_size("group") // 2
    tok = token_row.shape[0]
    d, n = w_gate.shape[1:]
    slab_rows, pw = ple_table.shape
    half, tq = d // 2, tok // 2
    per = ple_gate.shape[2]
    lanes = d // (2 * nz)
    dma = pltpu.SemaphoreType.DMA
    hbm, vmem = pl.BlockSpec(memory_space=pltpu.HBM), pl.BlockSpec(memory_space=pltpu.VMEM)
    stages = 2 * (SIDE - 1) + nz
    most = max(b - a for split in SPLITS for a, b in zip(split, split[1:]))
    rows_buf = pltpu.VMEM((nz, 2, SIDE, SIDE, 1, 2 * pw), F32)
    pairs = [
        (2, 2, 2, 4), (2, 2, 2, 4, 2), (2, 2, 2), (2, 2, 2, 2),
        (2, 2, 2), (2, 2, 2), (2, 2, 2, 4), (2, 2, 2, 4),
        (stages,), (stages,), (stages,),
    ]
    call = pl.pallas_call(
        functools.partial(body, nz, slab_rows),
        out_shape=jax.ShapeDtypeStruct((members, tok, d), BF),
        in_specs=[hbm] * 11,
        out_specs=vmem,
        scratch_shapes=[
            pltpu.VMEM((2, 16, tq, d), BF),
            pltpu.VMEM((tok, d), BF),
            pltpu.VMEM((d, n), BF),
            pltpu.VMEM((d, n), BF),
            pltpu.VMEM((n, d), BF),
            pltpu.VMEM((slab_rows, pw), BF),
            pltpu.VMEM((most * tq, n), BF),
            pltpu.VMEM((2, 2, 16, tq, half), BF),
            pltpu.VMEM((2, 2, 2, 4, tq, half // 2), BF),
            pltpu.VMEM((2, 2, 2, 4, tq, half), BF),
            pltpu.VMEM((2, 2, 2, tq, half // 2), BF),
            pltpu.VMEM((2, 2, 2, tq, half), BF),
            pltpu.VMEM((nz, 2, SIDE, SIDE, 1, tok), F32),
            rows_buf, rows_buf, rows_buf, rows_buf, rows_buf,
            pltpu.VMEM((nz, 2, 2, SIDE, SIDE, per, lanes), BF),
            pltpu.VMEM((3, 1, d), F32),
            pltpu.VMEM((1, tok), jnp.int32),
            pltpu.VMEM((1, tok), jnp.int32),
            pltpu.VMEM((1, slab_owner.shape[0]), jnp.int32),
            pltpu.VMEM((tok, pw), F32),
            dma((48,)),
        ] + [dma(shape) for shape in pairs for _ in range(2)],
        compiler_params=pltpu.CompilerParams(
            collective_id=0, has_side_effects=True, vmem_limit_bytes=40 * 1024 * 1024
        ),
        name="layer",
    )
    operands = (
        hidden.reshape(members, tok, d), w_gate[0], w_up[0], w_down[0], ple_gate[0].T, ple_proj[0], ple_table,
        norm_gains.reshape(3, 1, d), token_slab.reshape(1, tok), token_row.reshape(1, tok),
        slab_owner.reshape(1, -1),
    )
    out = call(*[pltpu.with_memory_space_constraint(v, pltpu.HBM) for v in operands])
    return out.reshape(members * tok, d)


def solution(mesh):
    return jax.shard_map(
        per_device,
        mesh=mesh,
        in_specs=(
            P("group", None),
            P(("group", "member"), None),
            P(("group", "member")),
            P(),
            P(("group", "member"), None),
            P(),
            P(None, None, "member"),
            P(None, None, "member"),
            P(None, "member", None),
            P(None, None, "member"),
            P(None, "member", None),
        ),
        out_specs=P("group", None),
        check_vma=False,
    )
```

time: 283 us -> 92.6 us (0.33)
  waiting for transfers between devices: 195 us -> 0 us
  Pallas kernels: 0 us -> 89.7 us
  matrix products: 25.3 us -> 0 us
  blocking collectives: 20.7 us -> 0 us
  between operations: 13.3 us -> 0.01 us
  other arithmetic: 13 us -> 0 us
  local copies, waits for them, and re-layouts: 10 us -> 2.71 us
  starting transfers between devices: 4.71 us -> 0 us
    all_gather x3 -> x0, waiting for transfers between devices: 146 us -> none  [the longest x1 60.6 us: per_device(): lax.all_gather(current.astype(jnp.bfloat16), 'member', axis=0, tiled=True)]
    pallas_call x0 -> x1, Pallas kernels: none -> 89.7 us  [per_device(): call(*[pltpu.with_memory_space_constraint(v, pltpu.HBM) for v in operands])]
    reduce_scatter x1 -> x0, waiting for transfers between devices: 37.6 us -> none  [per_device(): lax.psum_scatter(partial, 'member', scatter_dimension=0, tiled=True)]
    dot_general x5 -> x0, matrix products: 25.3 us -> none  [the longest x1 12.4 us: per_device(): jnp.dot(activated, w_down[0], preferred_element_type=jnp.float32)]
    all_to_all x1 -> x0, blocking collectives: 20.7 us -> none  [per_device(): lax.all_to_all(requests, ('group', 'member'), split_axis=0, concat_axis=0...]
    all_to_all x1 -> x0, waiting for transfers between devices: 10.7 us -> none  [per_device(): lax.all_to_all(served, ('group', 'member'), split_axis=0, concat_axis=0,...]
    reduce_sum x4 -> x0, other arithmetic: 7.88 us -> none  [the longest x2 5.47 us: norm_rows(): jnp.mean(values * values, axis=-1, keepdims=True) + epsilon]
    unnamed x19 -> x1, local copies, waits for them, and re-layouts: 7.92 us -> 2.71 us
  transfers between devices with their start and end apart: 5 -> 0, of which waited for: 5 -> 0; matrix products, arithmetic and copies ran while one was open for 4% -> 0% of each run, Pallas kernels for 0% -> 0%
where the time goes in v3:
time: 92.6 us; the launch traced here: 92.5 us
  Pallas kernels  89.7 us (97%)
  local copies, waits for them, and re-layouts  2.71 us (3%)
    pallas_call x1, Pallas kernels, per_device(): call(*[pltpu.with_memory_space_constraint(v, pltpu.HBM) for v in operands])  89.7 us
    unnamed x1, local copies, waits for them, and re-layouts  2.71 us

profile of v3, /device:TPU:0, one launch (start us, length us, event | category | flops | bytes accessed | tf_op | source)
XLA Modules:
  0.0 92.5 jit_solution(7454623489779121525)
XLA Ops:
  0.0 89.7 %layer.1 = bf16[16,96,2048]{2,1,0:T(8,128)(2,1)S(1)} custom-call(bf16[16,96,2048]{2,1,0:T(8,128)(2,1)} %bitcast.14, bf16[2048,512]{1,0:T(8,128)(2,1)} %bitcast.15, bf16[2048,512]{1,0:T(8,128)(2,1)} %bitcast.16, bf16[512,2048]{1,0:T(8,128)(2,1)} %bitcast.17, bf16[16,2048]{1,0:T(8,128)(2,1)} %bitcast.18, bf16[16,2048]{1,0:T(8,128)(2,1)} %bitcast.19, ...), custom_call_target="tpu_custom_call" | custom-call | tf_op jit(solution)/shard_map/layer/pallas_call | solution.py:528
  89.7 2.7 %copy.13 = bf16[1536,2048]{1,0:T(8,128)(2,1)} copy(bf16[1536,2048]{1,0:T(8,128)(2,1)S(1)} %bitcast.13) | data formatting | bytes 12582912

commit v4 on v3

--- a/solution.py
+++ b/solution.py
@@ -17,6 +17,7 @@
     (0, 1), (1, 0), (0, 3), (3, 0), (0, 0),
 ]
 SPLITS = ((0, 5, 11, 16), (0, 8, 16))
+DT = 1024
 WAVES = (2, 1, 3, 0)
 
 
@@ -41,7 +42,7 @@
     nz, slab_rows,
     hid_hbm, wg_hbm, wu_hbm, wd_hbm, pg_hbm, pp_hbm, table_hbm, gains_hbm, slab_hbm, rowid_hbm, owner_hbm,
     out,
-    hid, own, wg, wu, wd, table, act, part, r1a, r1b, r2a, r2b, ids, a0, a1, a2, a3, a4, wb,
+    hid, own, wg, wu, wd, table, act, part, r1a, r1b, r2a, r2b, ids, a0, a1, a2, wb,
     gains, slab, rowid, owner, looked,
     local_sem, ss1a, rs1a, ss1b, rs1b, ss2a, rs2a, ss2b, rs2b, sg1, rg1, sg2, rg2, sg3, rg3, sg4, rg4,
     sid, rid, sw, rw, sx, rx,
@@ -72,12 +73,14 @@
             return (lax.rem(z + off, nz) * 2 + c, m)
         return (z * 2 + 1 - c, m)
 
-    sizes = {"y": SIDE, "x": SIDE, "z": nz, "c": 2}
-    peers = [(a, o) for a in "yxzc" for o in range(1, sizes[a])]
+    shifts = [(dx, dy) for dx in range(SIDE) for dy in range(SIDE) if dx or dy]
+    members = [(g, at(dx, dy)) for dx, dy in shifts]
+    groups = [(lax.rem(g + o, 2 * nz), m) for o in range(1, 2 * nz)]
+    peers = members + groups
 
     barrier = pltpu.get_barrier_semaphore()
-    for a, o in peers:
-        pl.semaphore_signal(barrier, inc=1, device_id=along(a, o), device_id_type=MESH)
+    for peer in peers:
+        pl.semaphore_signal(barrier, inc=1, device_id=peer, device_id_type=MESH)
 
     locals_ = []
 
@@ -128,27 +131,31 @@
         started.append(copy)
         return copy
 
-    base = {"y": 0, "x": SIDE - 1, "z": 2 * SIDE - 2, "c": 2 * SIDE - 3 + nz}
-
-    def exchange(ref_of, dst, s, r, axis):
+    def exchange(devices, ref_of, dst, s, r, base):
         return [
-            launch(ref_of(o), dst, s.at[base[axis] + o - 1], r.at[base[axis] + o - 1], along(axis, o))
-            for o in range(1, sizes[axis])
+            launch(ref_of(*device), dst, s.at[base + i], r.at[base + i], device) for i, device in enumerate(devices)
         ]
 
     def arrive(copies):
         for copy in copies:
             copy.wait_recv()
 
-    def gather_ids(axis):
-        view = {"y": lambda: ids.at[z, c, x, y], "x": lambda: ids.at[z, c, x], "z": lambda: ids.at[z, c],
-                "c": lambda: ids.at[:, c]}[axis]()
-        return exchange(lambda o: view, view, sid, rid, axis)
-
-    def gather_w(axis):
-        view = {"y": lambda: wb.at[z, c, :, x, y], "x": lambda: wb.at[z, c, :, x], "z": lambda: wb.at[z, c],
-                "c": lambda: wb.at[:, c]}[axis]()
-        return exchange(lambda o: view, view, sw, rw, axis)
+    nm, ng = len(members), len(groups)
+
+    def same(devices, view, s, r, base):
+        return exchange(devices, lambda *_: view, view, s, r, base)
+
+    def gather_ids(stage):
+        if stage == 0:
+            return same(members, ids.at[z, c, x, y], sid, rid, 0)
+        return same(groups, ids.at[z, c], sid, rid, nm)
+
+    def gather_w(stage):
+        if stage == 0:
+            return same(members, wb.at[z, c, :, x, y], sw, rw, 0)
+        if stage == 1:
+            return same([along("z", o) for o in range(1, nz)], wb.at[z, c], sw, rw, nm)
+        return same([along("c", 1)], wb.at[:, c], sw, rw, nm + nz - 1)
 
     m1a, m1b, m2a, m2b = {}, {}, {}, {}
 
@@ -187,46 +194,38 @@
                 way = step.index(da)
                 send_1b(h, q, way, db, 1 - way)
 
-    def compute(q, i, between=lambda: None):
+    def normalise(q, i):
+        for k in range(SPLITS[q][i], SPLITS[q][i + 1]):
+            v = hid[q, k].astype(F32)
+            hid[q, k] = (v * rms_scale(v) * gains[0]).astype(BF)
+
+    def compute(q, i, between=lambda: None, following=None):
         k0, k1 = SPLITS[q][i], SPLITS[q][i + 1]
         rows = (k1 - k0) * tq
-        for k in range(k0, k1):
-            hid_in[q, k].wait()
         if (q, i) == (0, 0):
             in_gains.wait()
-        gain = gains[0]
-
-        @pl.loop(0, k1 - k0)
-        def _(k):
-            v = hid[q, k0 + k].astype(F32)
-            hid[q, k0 + k] = (v * rms_scale(v) * gain).astype(BF)
-
-        n = wg.shape[1]
-        tile = min(256, n)
-        if (q, i) == (0, 0):
+            for k in range(k0, k1):
+                hid_in[q, k].wait()
+            normalise(q, i)
             in_wg.wait()
             in_wu.wait()
-
-        @pl.loop(0, n // tile)
-        def _(j):
-            cols = pl.ds(pl.multiple_of(j * tile, 128), tile)
-            v = hid[q, k0:k1].reshape(rows, d)
-            gate = jnp.dot(v, wg[:, cols], preferred_element_type=F32)
-            up = jnp.dot(v, wu[:, cols], preferred_element_type=F32)
-            act[0:rows, cols] = (gelu(gate) * up).astype(BF)
-
+        if following:
+            for k in range(SPLITS[following[0]][following[1]], SPLITS[following[0]][following[1] + 1]):
+                hid_in[following[0], k].wait()
+        v = hid[q, k0:k1].reshape(rows, d)
+        gate = jnp.dot(v, wg[...], preferred_element_type=F32)
+        up = jnp.dot(v, wu[...], preferred_element_type=F32)
+        act[0:rows, :] = (gelu(gate) * up).astype(BF)
+        if following:
+            normalise(*following)
         between()
         if (q, i) == (0, 0):
             in_wd.wait()
-        dt = min(256, half)
+        dt = min(DT, half)
         per = half // dt
-
-        @pl.loop(0, 2 * per)
-        def _(j):
-            cols = pl.ds(pl.multiple_of(j * dt, 128), dt)
-            out_cols = pl.ds(pl.multiple_of(lax.rem(j, per) * dt, 128), dt)
-            v = jnp.dot(act[0:rows, :], wd[:, cols], preferred_element_type=F32).astype(BF)
-            part[j // per, q, k0:k1, :, out_cols] = v.reshape(k1 - k0, tq, dt)
+        for j in range(2 * per):
+            v = jnp.dot(act[0:rows, :], wd[:, j * dt:(j + 1) * dt], preferred_element_type=F32).astype(BF)
+            part[j // per, q, k0:k1, :, (j % per) * dt:(j % per + 1) * dt] = v.reshape(k1 - k0, tq, dt)
 
     def add_into(h, q, k, t, other):
         part[h, q, k, :, sub[t]] = (part[h, q, k, :, sub[t]].astype(F32) + other[...].astype(F32)).astype(BF)
@@ -277,21 +276,13 @@
             served = jnp.dot(pick, table[...], preferred_element_type=F32)
             a0[:, :, :, :, :, i * pw:(i + 1) * pw] = served.reshape(nz, 2, SIDE, SIDE, 1, pw)
 
-    def return_c():
-        a1[:, c] = a0[:, c]
-        return exchange(lambda o: a0.at[:, 1 - c], a1.at[:, c], sx, rx, "c")
-
-    def return_z():
-        a2[z] = a1[z]
-        return exchange(lambda o: a1.at[lax.rem(z + o, nz)], a2.at[z], sx, rx, "z")
-
-    def return_x():
-        a3[:, :, x] = a2[:, :, x]
-        return exchange(lambda o: a2.at[:, :, lax.rem(x + o, SIDE)], a3.at[:, :, x], sx, rx, "x")
-
-    def return_y():
-        a4[:, :, :, y] = a3[:, :, :, y]
-        return exchange(lambda o: a3.at[:, :, :, lax.rem(y + o, SIDE)], a4.at[:, :, :, y], sx, rx, "y")
+    def send_rows(stage):
+        if stage == 0:
+            a1[:, :, x, y] = a0[:, :, x, y]
+            return exchange(
+                members, lambda _, mm: a0.at[:, :, mm // SIDE, lax.rem(mm, SIDE)], a1.at[:, :, x, y], sx, rx, 0)
+        a2[z, c] = a1[z, c]
+        return exchange(groups, lambda gg, _: a1.at[gg // 2, lax.rem(gg, 2)], a2.at[z, c], sx, rx, nm)
 
     def look():
         target_col = diagonal_column(target_row, tok)
@@ -302,7 +293,7 @@
         rows = jnp.zeros((tok, pw), F32)
         for i in range(2):
             pick = jnp.where(owners & (second == float(i)), 1.0, 0.0).astype(BF)
-            rows_i = a4[:, :, :, :, :, i * pw:(i + 1) * pw].reshape(ndev, pw).astype(BF)
+            rows_i = a2[:, :, :, :, :, i * pw:(i + 1) * pw].reshape(ndev, pw).astype(BF)
             rows += jnp.dot(pick, rows_i, preferred_element_type=F32)
         looked[...] = rows * float(pw) ** 0.5
 
@@ -378,58 +369,44 @@
                 g4[h, q, way, db] = launch(view, view, sg4.at[h, q, way, db], rg4.at[h, q, way, db],
                                            along(first_axis[h], step[way]))
 
-    fi = gather_ids("y")
+    fi = gather_ids(0)
     for copy in in_w:
         copy.wait()
-    fw = gather_w("y")
-    box = {}
-
-    def early():
-        arrive(fi)
-        box["i"] = gather_ids("x")
-        arrive(fw)
-        box["w"] = gather_w("x")
-
-    compute(0, 0, early)
+    fw = gather_w(0)
+    compute(0, 0, following=(0, 1))
     send_ready(0, 0)
-    compute(0, 1)
+    arrive(fi)
+    fi = gather_ids(1)
+    compute(0, 1, following=(0, 2))
     send_ready(0, 1)
     relay_1(0, 2)
-    arrive(box["i"])
-    fi = gather_ids("z")
-    arrive(box["w"])
-    fw = gather_w("z")
-    compute(0, 2)
+    arrive(fi)
+    serve()
+    fx = send_rows(0)
+    arrive(fw)
+    fw = gather_w(1)
+    compute(0, 2, following=(1, 0))
     send_ready(0, 2)
     relay_1(0, 1)
     relay_1(0, 3)
     relay_1(0, 0)
-    arrive(fi)
-    fi = gather_ids("c")
-    compute(1, 0)
+    compute(1, 0, following=(1, 1))
     sum_1(0, 2)
     send_ready(1, 0)
-    arrive(fi)
-    serve()
-    fx = return_c()
+    arrive(fx)
+    fx = send_rows(1)
     compute(1, 1)
     sum_1(0, 1)
     sum_1(0, 3)
-    arrive(fx)
-    fx = return_z()
     relay_2(0)
     send_ready(1, 1)
+    arrive(fw)
+    fw = gather_w(2)
     relay_1(1, 2)
-    arrive(fx)
-    fx = return_x()
     relay_1(1, 1)
     relay_1(1, 3)
     relay_1(1, 0)
-    arrive(fw)
-    fw = gather_w("c")
     sum_1(0, 0)
-    arrive(fx)
-    fx = return_y()
     sum_1(1, 2)
     arrive(fx)
     in_own.wait()
@@ -479,7 +456,7 @@
     lanes = d // (2 * nz)
     dma = pltpu.SemaphoreType.DMA
     hbm, vmem = pl.BlockSpec(memory_space=pltpu.HBM), pl.BlockSpec(memory_space=pltpu.VMEM)
-    stages = 2 * (SIDE - 1) + nz
+    stages = SIDE * SIDE + 2 * nz
     most = max(b - a for split in SPLITS for a, b in zip(split, split[1:]))
     rows_buf = pltpu.VMEM((nz, 2, SIDE, SIDE, 1, 2 * pw), F32)
     pairs = [
@@ -506,7 +483,7 @@
             pltpu.VMEM((2, 2, 2, tq, half // 2), BF),
             pltpu.VMEM((2, 2, 2, tq, half), BF),
             pltpu.VMEM((nz, 2, SIDE, SIDE, 1, tok), F32),
-            rows_buf, rows_buf, rows_buf, rows_buf, rows_buf,
+            rows_buf, rows_buf, rows_buf,
             pltpu.VMEM((nz, 2, 2, SIDE, SIDE, per, lanes), BF),
             pltpu.VMEM((3, 1, d), F32),
             pltpu.VMEM((1, tok), jnp.int32),

time: 92.6 us -> 87.7 us (0.947)
  Pallas kernels: 89.7 us -> 84.4 us
    pallas_call x1, Pallas kernels: 89.7 us -> 84.4 us  [per_device(): call(*[pltpu.with_memory_space_constraint(v, pltpu.HBM) for v in operands])]
where the time goes in v4:
time: 87.7 us; the launch traced here: 87.2 us
  Pallas kernels  84.4 us (96%)
  local copies, waits for them, and re-layouts  2.71 us (3%)
    pallas_call x1, Pallas kernels, per_device(): call(*[pltpu.with_memory_space_constraint(v, pltpu.HBM) for v in operands])  84.4 us
    unnamed x1, local copies, waits for them, and re-layouts  2.71 us

profile of v4, /device:TPU:0, one launch (start us, length us, event | category | flops | bytes accessed | tf_op | source)
XLA Modules:
  0.0 87.2 jit_solution(9916808841505115046)
XLA Ops:
  0.0 84.4 %layer.1 = bf16[16,96,2048]{2,1,0:T(8,128)(2,1)S(1)} custom-call(bf16[16,96,2048]{2,1,0:T(8,128)(2,1)} %bitcast.14, bf16[2048,512]{1,0:T(8,128)(2,1)} %bitcast.15, bf16[2048,512]{1,0:T(8,128)(2,1)} %bitcast.16, bf16[512,2048]{1,0:T(8,128)(2,1)} %bitcast.17, bf16[16,2048]{1,0:T(8,128)(2,1)} %bitcast.18, bf16[16,2048]{1,0:T(8,128)(2,1)} %bitcast.19, ...), custom_call_target="tpu_custom_call" | custom-call | tf_op jit(solution)/shard_map/layer/pallas_call | solution.py:505
  84.4 2.7 %copy.13 = bf16[1536,2048]{1,0:T(8,128)(2,1)} copy(bf16[1536,2048]{1,0:T(8,128)(2,1)S(1)} %bitcast.13) | data formatting | bytes 12582912

commit v5 on v4

--- a/solution.py
+++ b/solution.py
@@ -16,7 +16,7 @@
     (1, 1), (1, 3), (3, 1), (3, 3), (0, 2), (2, 0),
     (0, 1), (1, 0), (0, 3), (3, 0), (0, 0),
 ]
-SPLITS = ((0, 5, 11, 16), (0, 8, 16))
+SPLITS = ((0, 1, 5, 11, 16), (0, 8, 16))
 DT = 1024
 WAVES = (2, 1, 3, 0)
 
@@ -98,7 +98,7 @@
         for k in range(k0, k1):
             hid_in[q, k] = local(hid_hbm.at[at(*ORDER[k]), toks[q]], hid.at[q, k])
 
-    load_hidden(0, 0, 5)
+    load_hidden(0, 0, 1)
     lane0 = pl.multiple_of(g * lanes, 128)
     in_w = [
         local(pg_hbm.at[:, pl.ds(lane0, lanes)], wb.at[z, c, 0, x, y]),
@@ -107,7 +107,7 @@
     in_wg = local(wg_hbm, wg)
     in_wu = local(wu_hbm, wu)
     in_wd = local(wd_hbm, wd)
-    load_hidden(0, 5, 16)
+    load_hidden(0, 1, 16)
     load_hidden(1, 0, 16)
     in_table = local(table_hbm, table)
     in_own = local(hid_hbm.at[m], own)
@@ -130,6 +130,13 @@
         copy.start()
         started.append(copy)
         return copy
+
+    drained = []
+
+    def drain(upto):
+        for copy in started[len(drained):upto]:
+            copy.wait_send()
+            drained.append(copy)
 
     def exchange(devices, ref_of, dst, s, r, base):
         return [
@@ -274,7 +281,7 @@
         for i, wanted in enumerate((id0, id1)):
             pick = jnp.where(row_iota == wanted, 1.0, 0.0).astype(BF)
             served = jnp.dot(pick, table[...], preferred_element_type=F32)
-            a0[:, :, :, :, :, i * pw:(i + 1) * pw] = served.reshape(nz, 2, SIDE, SIDE, 1, pw)
+            a0[:, :, :, :, i, :] = served.astype(BF).reshape(nz, 2, SIDE, SIDE, pw)
 
     def send_rows(stage):
         if stage == 0:
@@ -293,7 +300,7 @@
         rows = jnp.zeros((tok, pw), F32)
         for i in range(2):
             pick = jnp.where(owners & (second == float(i)), 1.0, 0.0).astype(BF)
-            rows_i = a2[:, :, :, :, :, i * pw:(i + 1) * pw].reshape(ndev, pw).astype(BF)
+            rows_i = a2[:, :, :, :, i, :].reshape(ndev, pw)
             rows += jnp.dot(pick, rows_i, preferred_element_type=F32)
         looked[...] = rows * float(pw) ** 0.5
 
@@ -373,20 +380,25 @@
     for copy in in_w:
         copy.wait()
     fw = gather_w(0)
-    compute(0, 0, following=(0, 1))
+    compute(0, 0)
     send_ready(0, 0)
+    for k in range(SPLITS[0][1], SPLITS[0][2]):
+        hid_in[0, k].wait()
+    normalise(0, 1)
+    compute(0, 1, following=(0, 2))
+    send_ready(0, 1)
     arrive(fi)
     fi = gather_ids(1)
-    compute(0, 1, following=(0, 2))
-    send_ready(0, 1)
+    compute(0, 2, following=(0, 3))
+    send_ready(0, 2)
     relay_1(0, 2)
     arrive(fi)
     serve()
     fx = send_rows(0)
     arrive(fw)
     fw = gather_w(1)
-    compute(0, 2, following=(1, 0))
-    send_ready(0, 2)
+    compute(0, 3, following=(1, 0))
+    send_ready(0, 3)
     relay_1(0, 1)
     relay_1(0, 3)
     relay_1(0, 0)
@@ -413,6 +425,7 @@
     look()
     arrive(fw)
     finish(0)
+    n0 = len(started)
     publish(0)
     spread(0, 0)
     sum_1(1, 1)
@@ -425,8 +438,10 @@
     settle(0)
     spread(0, 2)
     finish(1)
+    n1 = len(started)
     publish(1)
     spread(1, 0)
+    drain(n0)
     forward(0, 0)
     pass_on(1)
     spread(1, 1)
@@ -436,11 +451,14 @@
     settle(1)
     spread(1, 2)
     forward(0, 2)
-    for db in (0, 1, 3, 2):
+    n2 = len(started)
+    forward(1, 0)
+    drain(n1)
+    for db in (1, 3, 2):
         forward(1, db)
+    drain(n2)
     arrive(g4.values())
-    for copy in started:
-        copy.wait_send()
+    drain(len(started))
 
 
 def per_device(
@@ -458,7 +476,7 @@
     hbm, vmem = pl.BlockSpec(memory_space=pltpu.HBM), pl.BlockSpec(memory_space=pltpu.VMEM)
     stages = SIDE * SIDE + 2 * nz
     most = max(b - a for split in SPLITS for a, b in zip(split, split[1:]))
-    rows_buf = pltpu.VMEM((nz, 2, SIDE, SIDE, 1, 2 * pw), F32)
+    rows_buf = pltpu.VMEM((nz, 2, SIDE, SIDE, 2, pw), BF)
     pairs = [
         (2, 2, 2, 4), (2, 2, 2, 4, 2), (2, 2, 2), (2, 2, 2, 2),
         (2, 2, 2), (2, 2, 2), (2, 2, 2, 4), (2, 2, 2, 4),

time: 87.7 us -> 85.5 us (0.975)
  Pallas kernels: 84.4 us -> 82.5 us
    pallas_call x1, Pallas kernels: 84.4 us -> 82.5 us  [per_device(): call(*[pltpu.with_memory_space_constraint(v, pltpu.HBM) for v in operands])]
where the time goes in v5:
time: 85.5 us; the launch traced here: 85.2 us
  Pallas kernels  82.5 us (96%)
  local copies, waits for them, and re-layouts  2.71 us (3%)
    pallas_call x1, Pallas kernels, per_device(): call(*[pltpu.with_memory_space_constraint(v, pltpu.HBM) for v in operands])  82.5 us
    unnamed x1, local copies, waits for them, and re-layouts  2.71 us

profile of v5, /device:TPU:0, one launch (start us, length us, event | category | flops | bytes accessed | tf_op | source)
XLA Modules:
  0.0 85.2 jit_solution(17431383767084954649)
XLA Ops:
  0.0 82.5 %layer.1 = bf16[16,96,2048]{2,1,0:T(8,128)(2,1)S(1)} custom-call(bf16[16,96,2048]{2,1,0:T(8,128)(2,1)} %bitcast.14, bf16[2048,512]{1,0:T(8,128)(2,1)} %bitcast.15, bf16[2048,512]{1,0:T(8,128)(2,1)} %bitcast.16, bf16[512,2048]{1,0:T(8,128)(2,1)} %bitcast.17, bf16[16,2048]{1,0:T(8,128)(2,1)} %bitcast.18, bf16[16,2048]{1,0:T(8,128)(2,1)} %bitcast.19, ...), custom_call_target="tpu_custom_call" | custom-call | tf_op jit(solution)/shard_map/layer/pallas_call | solution.py:523
  82.5 2.7 %copy.13 = bf16[1536,2048]{1,0:T(8,128)(2,1)} copy(bf16[1536,2048]{1,0:T(8,128)(2,1)S(1)} %bitcast.13) | data formatting | bytes 12582912

commit v6 on v5

--- a/solution.py
+++ b/solution.py
@@ -402,8 +402,8 @@
     relay_1(0, 1)
     relay_1(0, 3)
     relay_1(0, 0)
+    sum_1(0, 2)
     compute(1, 0, following=(1, 1))
-    sum_1(0, 2)
     send_ready(1, 0)
     arrive(fx)
     fx = send_rows(1)

time: 85.5 us -> 85.5 us (level)
  no operation moved by 1% of the time
where the time goes in v6:
time: 85.5 us; the launch traced here: 85.2 us
  Pallas kernels  82.5 us (96%)
  local copies, waits for them, and re-layouts  2.71 us (3%)
    pallas_call x1, Pallas kernels, per_device(): call(*[pltpu.with_memory_space_constraint(v, pltpu.HBM) for v in operands])  82.5 us
    unnamed x1, local copies, waits for them, and re-layouts  2.71 us

profile of v6, /device:TPU:0, one launch (start us, length us, event | category | flops | bytes accessed | tf_op | source)
XLA Modules:
  0.0 85.2 jit_solution(5153893851415166150)
XLA Ops:
  0.0 82.5 %layer.1 = bf16[16,96,2048]{2,1,0:T(8,128)(2,1)S(1)} custom-call(bf16[16,96,2048]{2,1,0:T(8,128)(2,1)} %bitcast.14, bf16[2048,512]{1,0:T(8,128)(2,1)} %bitcast.15, bf16[2048,512]{1,0:T(8,128)(2,1)} %bitcast.16, bf16[512,2048]{1,0:T(8,128)(2,1)} %bitcast.17, bf16[16,2048]{1,0:T(8,128)(2,1)} %bitcast.18, bf16[16,2048]{1,0:T(8,128)(2,1)} %bitcast.19, ...), custom_call_target="tpu_custom_call" | custom-call | tf_op jit(solution)/shard_map/layer/pallas_call | solution.py:523
  82.5 2.7 %copy.13 = bf16[1536,2048]{1,0:T(8,128)(2,1)} copy(bf16[1536,2048]{1,0:T(8,128)(2,1)S(1)} %bitcast.13) | data formatting | bytes 12582912
